TPU v7x, 256 devices: a whole 4x4x8 slice. The times are simulated.
256 devices in a mesh: cell: 32 (over y_hi, z, core), brick: 8 (over x, y_lo).
Axes of the slice: x: 4, y: 4 (y_hi: 2, y_lo: 2; y = y_hi * 2 + y_lo), z: 8, core: 2. Of those that a mesh axis runs over, the one named last changes fastest.
Arguments:
- features: bfloat16 [32, 8, 128, 256], P('cell', 'brick'), may hold values from -6 to 6
- species: int32 [32, 8, 128], P('cell', 'brick'), may hold values from 0 to 3
- species_table: bfloat16 [4, 256], replicated, may hold values from -3 to 3
- neighbours: int32 [32, 8, 64, 128], P('cell', 'brick'), may hold values from 0 to 383
- counts: int32 [32, 8, 128], P('cell', 'brick'), may hold values from 1 to 64
- send_lists: int32 [32, 8, 8, 32], P('cell', 'brick'), may hold values from 0 to 127
- distances: float32 [32, 8, 64, 128], P('cell', 'brick'), may hold values from 0.05 to 1
- head_decay: float32 [8], replicated, may hold values from 0.25 to 4
- norm_gain: float32 [256], replicated, may hold values from 0.5 to 1.5
- readout: float32 [256], replicated, may hold values from -0.375 to 0.375
- targets: float32 [32, 8, 128], P('cell', 'brick'), may hold values from -6 to 6
- master: float32 [4, 256, 256], P(None, 'cell'), as said below
- moment: float32 [4, 256, 256], P(None, 'cell'), may hold values from -3 to 3
- second: float32 [4, 256, 256], P(None, 'cell'), may hold values from 0.1 to 1
Outputs:
- energies: float32 [32, 8, 128], P('cell', 'brick')
- moment_new: float32 [4, 256, 256], P(None, 'cell')
- second_new: float32 [4, 256, 256], P(None, 'cell')
- adam_step: float32 [4, 256, 256], P(None, 'cell')
Inputs may be any that keep to these rules, and one draw needn't show every extreme that they name: `master`: projection entries lie within -48 * 256^-0.5 and 48 * 256^-0.5.
All inputs are finite; a program needn't handle non-finite values.
Results may differ from a plain program's by a relative error of at most 0.0045.
The roundings to bfloat16 on the way count: a program that leaves them out, or rounds other values in their place, can miss the bound.
Values may be sent and summed in bfloat16 or wider, within the bound.
A program may use at most 64 MiB of HBM per device.

v0:
```python
import math

import jax
import jax.numpy as jnp
from jax import lax
from jax.sharding import PartitionSpec as P

TILE = 128


loss_weight = 0.0625
epsilon_norm = 1e-06


def silu_slope(inputs):
    sigmoid_val = jax.nn.sigmoid(inputs)
    return sigmoid_val * (1.0 + inputs * (1.0 - sigmoid_val))


def normalize(embedded, norm_gain):
    rms_scale = lax.rsqrt(jnp.mean(embedded * embedded, axis=-1, keepdims=True) + epsilon_norm)
    return (embedded * rms_scale * norm_gain).astype(jnp.bfloat16)


def brick_sweep(
    query,
    key_table,
    value_table,
    embedded,
    neighbour_rows,
    local_count,
    local_dist,
    local_target,
    out_proj,
    head_decay,
    readout,
):
    atom_count, model_width = query.shape
    head_count = head_decay.shape[0]
    head_size = model_width // head_count
    slot_count = neighbour_rows.shape[0]
    score_scale = 1.0 / math.sqrt(head_size)
    table_rows = key_table.shape[0]

    def tile_step(grad_carry, tile_index):
        key_grads, value_grads = grad_carry
        key_rows = key_table[neighbour_rows].reshape(slot_count, TILE, head_count, head_size)
        value_rows = value_table[neighbour_rows].reshape(slot_count, TILE, head_count, head_size)
        query_heads = query.reshape(TILE, head_count, head_size)
        is_valid = (jnp.arange(slot_count)[:, None] < local_count[None, :])[:, :, None]
        score = (
            jnp.einsum("ahd,kahd->kah", query_heads, key_rows, preferred_element_type=jnp.float32)
            * score_scale
        )
        score = score - head_decay[None, None, :] * local_dist[:, :, None]
        score = jnp.where(is_valid, score, -1e30)
        row_max = jnp.max(score, axis=0, keepdims=True)
        exp_terms = jnp.where(is_valid, jnp.exp(score - row_max), 0.0)
        attention = exp_terms / jnp.sum(exp_terms, axis=0, keepdims=True)
        attention_half = attention.astype(jnp.bfloat16)
        attended = jnp.einsum(
            "kah,kahd->ahd", attention_half, value_rows, preferred_element_type=jnp.float32
        )
        attended = attended.astype(jnp.bfloat16).reshape(TILE, model_width)
        updated = embedded + jnp.dot(attended, out_proj, preferred_element_type=jnp.float32)
        energy = jnp.sum(readout * jax.nn.silu(updated), axis=-1)
        grad_energy = loss_weight * (energy - local_target)
        grad_updated = (grad_energy[:, None] * readout * silu_slope(updated)).astype(jnp.bfloat16)
        grad_attended = jnp.einsum(
            "ad,cd->ac", grad_updated, out_proj, preferred_element_type=jnp.float32
        ).astype(jnp.bfloat16)
        grad_att_heads = grad_attended.reshape(TILE, head_count, head_size)
        grad_weights = jnp.einsum(
            "ahd,kahd->kah", grad_att_heads, value_rows, preferred_element_type=jnp.float32
        )
        grad_score = attention * (
            grad_weights - jnp.sum(attention * grad_weights, axis=0, keepdims=True)
        )
        grad_score = grad_score.astype(jnp.bfloat16)
        grad_query = (
            jnp.einsum("kah,kahd->ahd", grad_score, key_rows, preferred_element_type=jnp.float32)
            * score_scale
        )
        grad_query = grad_query.astype(jnp.bfloat16).reshape(TILE, model_width)
        key_edge = (
            grad_score.astype(jnp.float32)[..., None]
            * query_heads.astype(jnp.float32)[None]
            * score_scale
        )
        value_edge = (
            attention_half.astype(jnp.float32)[..., None] * grad_att_heads.astype(jnp.float32)[None]
        )
        flattened_rows = neighbour_rows.reshape(-1)
        key_grads = key_grads.at[flattened_rows].add(key_edge.reshape(-1, model_width))
        value_grads = value_grads.at[flattened_rows].add(value_edge.reshape(-1, model_width))
        return ((key_grads, value_grads), (energy, attended, grad_updated, grad_query))

    start_grads = (
        jnp.zeros((table_rows, model_width), jnp.float32),
        jnp.zeros((table_rows, model_width), jnp.float32),
    )
    (key_grads, value_grads), stacked = lax.scan(
        tile_step, start_grads, jnp.arange(atom_count // TILE, dtype=jnp.int32)
    )
    energy, attended, grad_updated, grad_query = stacked
    return (
        key_grads,
        value_grads,
        energy.reshape(atom_count),
        attended.reshape(atom_count, model_width),
        grad_updated.reshape(atom_count, model_width),
        grad_query.reshape(atom_count, model_width),
    )


def body(
    features,
    species,
    species_table,
    neighbours,
    counts,
    send_lists,
    distances,
    head_decay,
    norm_gain,
    readout,
    targets,
    master,
    moment,
    second,
):
    local_feat = features[0, 0]
    local_species = species[0, 0]
    neighbour_rows = neighbours[0, 0]
    local_count = counts[0, 0]
    send_rows = send_lists[0, 0]
    local_dist = distances[0, 0]
    local_target = targets[0, 0]
    atom_count, model_width = local_feat.shape
    bricks, ghost_position = send_rows.shape
    species_count = species_table.shape[0]
    picked = (local_species[:, None] == jnp.arange(species_count)[None, :]).astype(jnp.bfloat16)
    embedded = local_feat.astype(jnp.float32) + jnp.dot(
        picked, species_table, preferred_element_type=jnp.float32
    )
    normed_features = normalize(embedded, norm_gain)
    attention_weights = lax.all_gather(master.astype(jnp.bfloat16), "cell", axis=1, tiled=True)
    projected = jnp.einsum(
        "pe,mer->mpr", normed_features, attention_weights[0:3], preferred_element_type=jnp.float32
    ).astype(jnp.bfloat16)
    flat_send = send_rows.reshape(-1)
    parcel = projected[1:3][:, flat_send].reshape(2, bricks, ghost_position, model_width)
    arrived = lax.all_to_all(parcel, "brick", split_axis=1, concat_axis=1, tiled=True)
    ghost_keys = arrived[0].reshape(-1, model_width)
    ghost_values = arrived[1].reshape(-1, model_width)
    key_table = jnp.concatenate([projected[1], ghost_keys], axis=0)
    value_table = jnp.concatenate([projected[2], ghost_values], axis=0)
    key_grads, value_grads, energy, attended, grad_updated, grad_query = brick_sweep(
        projected[0],
        key_table,
        value_table,
        embedded,
        neighbour_rows,
        local_count,
        local_dist,
        local_target,
        attention_weights[3],
        head_decay,
        readout,
    )
    ghost_grads = jnp.stack([key_grads[atom_count:], value_grads[atom_count:]]).reshape(
        2, bricks, ghost_position, model_width
    )
    returned = lax.all_to_all(
        ghost_grads.astype(jnp.bfloat16), "brick", split_axis=1, concat_axis=1, tiled=True
    ).astype(ghost_grads.dtype)
    local_portion = jnp.stack([key_grads[:atom_count], value_grads[:atom_count]])
    totals = (
        local_portion.at[:, flat_send]
        .add(returned.reshape(2, -1, model_width))
        .astype(jnp.bfloat16)
    )
    grad_q = jnp.einsum(
        "ac,ad->cd", normed_features, grad_query, preferred_element_type=jnp.float32
    )
    key_gradient = jnp.einsum(
        "ac,ad->cd", normed_features, totals[0], preferred_element_type=jnp.float32
    )
    grad_v = jnp.einsum("ac,ad->cd", normed_features, totals[1], preferred_element_type=jnp.float32)
    grad_o = jnp.einsum("ac,ad->cd", attended, grad_updated, preferred_element_type=jnp.float32)
    grads = jnp.stack([grad_q, key_gradient, grad_v, grad_o])
    summed = lax.psum(grads.astype(jnp.bfloat16), "brick")
    owned = lax.psum_scatter(summed, "cell", scatter_dimension=1, tiled=True).astype(jnp.float32)
    moment_new = 0.9 * moment + 0.1 * owned
    second_new = 0.999 * second + 0.001 * owned * owned
    adam_step = moment_new / (jnp.sqrt(second_new) + 1e-08)
    return (energy[None, None, :], moment_new, second_new, adam_step)


def solution(mesh):
    return jax.shard_map(
        body,
        mesh=mesh,
        in_specs=(
            P("cell", "brick", None, None),
            P("cell", "brick", None),
            P(),
            P("cell", "brick", None, None),
            P("cell", "brick", None),
            P("cell", "brick", None, None),
            P("cell", "brick", None, None),
            P(),
            P(),
            P(),
            P("cell", "brick", None),
            P(None, "cell", None),
            P(None, "cell", None),
            P(None, "cell", None),
        ),
        out_specs=(
            P("cell", "brick", None),
            P(None, "cell", None),
            P(None, "cell", None),
            P(None, "cell", None),
        ),
        check_vma=False,
    )
```

profile of v0, /device:TPU:16, one launch (start us, length us, event | category | flops | bytes accessed | tf_op | source)
XLA Modules:
  0.0 491.3 jit_solution(7539827670805211175)
XLA Ops:
  7.2 0.8 reshape_squeeze.17
  8.0 0.8 convert_element_type.79
  8.7 1.2 multiply_reduce_fusion.5
  9.9 43.4 %all_gather.3 = bf16[4,256,256]{2,1,0:T(8,128)(2,1)S(1)} all-gather(bf16[4,8,256]{2,1,0:T(8,128)(2,1)S(1)} %convert_element_type.79), channel_id=1, replica_groups=mesh['cell'=32,'brick'=8] {'cell'}, dimensions={1}, use_global_device_ids=true | all-gather | bytes 540672 | tf_op jit(solution)/shard_map/all_gather | solution.py:147
  53.3 0.8 multiply_convert_fusion.2
  54.1 0.2 fusion.10
  54.5 1.2 gather_fusion
  55.7 0.7 copy.53
  56.4 5.9 %all-to-all-start = ((bf16[2,8,32,256]{3,2,0,1:T(8,128)(2,1)}), bf16[2,8,32,256]{3,2,0,1:T(8,128)(2,1)S(1)}, u32[]{:S(2)}, u32[]{:S(2)}) async-start(bf16[2,8,32,256]{3,2,0,1:T(8,128)(2,1)} %copy.53), calls=%async_computation | async-start | bytes 524288 | tf_op jit(solution)/shard_map/all_to_all | solution.py:153
  62.4 0.8 compare_select_fusion
  63.2 0.7 iota_compare_fusion.2
  64.0 0.8 fusion.37
  64.8 5.0 %all-to-all-done = bf16[2,8,32,256]{3,2,0,1:T(8,128)(2,1)S(1)} async-done(((bf16[2,8,32,256]{3,2,0,1:T(8,128)(2,1)}), bf16[2,8,32,256]{3,2,0,1:T(8,128)(2,1)S(1)}, u32[]{:S(2)}, u32[]{:S(2)}) %all-to-all-start) | async-done | bytes 262176 | tf_op jit(solution)/shard_map/all_to_all | solution.py:153
  69.9 32.9 %gather_fusion.1 = bf16[8192,256]{1,0:T(8,128)(2,1)} fusion(bf16[384,256]{1,0:T(8,128)(2,1)S(1)} %get-tuple-element.81, s32[8192]{0:T(1024)S(1)} %fusion.37), kind=kCustom, calls=%fused_computation.1 | custom fusion | bytes 8421376 | tf_op jit(solution)/shard_map/while/body/eval_jaxpr/gather | solution.py:47
  102.8 6.4 %copy.55 = bf16[8192,256]{0,1:T(8,128)(2,1)} copy(bf16[8192,256]{1,0:T(8,128)(2,1)} %gather_fusion.1) | data formatting | bytes 8388608 | tf_op jit(solution)/shard_map/while/body/eval_jaxpr/gather | solution.py:47
  109.2 5.3 %copy.103 = bf16[32,8,64,128]{3,2,1,0:T(8,128)(2,1)} copy(bf16[32,8,64,128]{3,1,2,0:T(8,128)(2,1)} %bitcast.154) | data formatting | bytes 8388608
  114.5 32.9 %gather_fusion.2 = bf16[8192,256]{1,0:T(8,128)(2,1)} fusion(bf16[384,256]{1,0:T(8,128)(2,1)S(1)} %get-tuple-element.82, s32[8192]{0:T(1024)S(1)} %fusion.37), kind=kCustom, calls=%fused_computation.2 | custom fusion | bytes 8421376 | tf_op jit(solution)/shard_map/while/body/eval_jaxpr/gather | solution.py:48
  147.4 6.7 %copy.58 = bf16[8192,256]{0,1:T(8,128)(2,1)} copy(bf16[8192,256]{1,0:T(8,128)(2,1)} %gather_fusion.2) | data formatting | bytes 8388608 | tf_op jit(solution)/shard_map/while/body/eval_jaxpr/gather | solution.py:48
  154.2 5.5 %copy.104 = bf16[32,8,64,128]{3,2,1,0:T(8,128)(2,1)} copy(bf16[32,8,64,128]{3,1,2,0:T(8,128)(2,1)} %bitcast.155) | data formatting | bytes 8388608
  159.7 1.2 multiply_reduce_fusion.3
  160.9 1.1 convert_convert_fusion
  162.0 4.0 multiply_reduce_fusion.2
  166.0 0.3 multiply_reduce_fusion.4
  166.3 0.2 convolution_convert_fusion.5
  166.7 3.4 multiply_reduce_fusion.1
  170.1 1.1 broadcast_multiply_fusion
  171.2 22.6 %copy.118 = f32[32,8,64,128]{3,1,2,0:T(8,128)} copy(f32[32,8,64,128]{3,2,1,0:T(8,128)S(1)} %bitcast.150) | data formatting | bytes 16777216
  193.8 9.0 %copy.61 = f32[8192,256]{1,0:T(8,128)} copy(f32[8192,256]{0,1:T(8,128)} %bitcast.152) | data formatting | bytes 16777216 | tf_op jit(solution)/shard_map/while/body/eval_jaxpr/mul | solution.py:91
  202.8 44.7 %scatter_custom_fusion.1 = f32[384,256]{1,0:T(8,128)S(1)} fusion(s32[8192]{0:T(1024)S(1)} %bitcast.169, f32[8192,256]{1,0:T(8,128)} %copy.61, f32[]{:T(128)} %constant.16.clone.1), kind=kCustom, calls=%fused_computation.51 | custom fusion | flops 2097152 | bytes 393728 | tf_op jit(solution)/shard_map/while/body/eval_jaxpr/scatter-add | solution.py:95
  247.6 0.2 bitcast_convert_fusion
  247.8 1.2 multiply_multiply_fusion
  249.1 10.9 %copy.119 = f32[32,8,64,128]{3,1,2,0:T(8,128)} copy(f32[32,8,64,128]{3,2,1,0:T(8,128)S(1)} %bitcast.151) | data formatting | bytes 16777216
  259.9 9.0 %copy.60 = f32[8192,256]{1,0:T(8,128)} copy(f32[8192,256]{0,1:T(8,128)} %bitcast.153) | data formatting | bytes 16777216 | tf_op jit(solution)/shard_map/while/body/eval_jaxpr/mul | solution.py:86
  268.9 44.9 %scatter_custom_fusion = f32[384,256]{1,0:T(8,128)S(1)} fusion(s32[8192]{0:T(1024)S(1)} %bitcast.170, f32[8192,256]{1,0:T(8,128)} %copy.60, f32[]{:T(128)} %constant.16.clone.1), kind=kCustom, calls=%fused_computation.53 | custom fusion | flops 2097152 | bytes 393728 | tf_op jit(solution)/shard_map/while/body/eval_jaxpr/scatter-add | solution.py:94
  313.9 4.0 multiply_reduce_fusion
  318.2 0.7 pad_maximum_fusion.2
  318.9 3.4 all-to-all-start.1
  322.4 0.2 fusion.11
  322.6 0.2 fusion.14
  322.8 6.4 %all-to-all-done.1 = bf16[2,8,32,256]{3,2,0,1:T(8,128)(2,1)S(1)} async-done(((bf16[2,8,32,256]{3,2,0,1:T(8,128)(2,1)}), bf16[2,8,32,256]{3,2,0,1:T(8,128)(2,1)S(1)}, u32[]{:S(2)}, u32[]{:S(2)}) %all-to-all-start.1) | async-done | bytes 262176 | tf_op jit(solution)/shard_map/all_to_all | solution.py:174
  329.3 0.4 copy.66
  329.7 8.9 %scatter_fusion = f32[2,128,256]{2,0,1:T(2,128)S(1)} fusion(f32[2,128,256]{2,0,1:T(2,128)S(1)} %copy.65, s32[256]{0:T(256)S(1)} %bitcast.172, f32[256,2,256]{2,1,0:T(2,128)S(1)} %copy.66), kind=kCustom, calls=%fused_computation.5 | custom fusion | flops 131072 | bytes 1573888 | tf_op jit(solution)/shard_map/scatter-add | solution.py:180
  339.4 0.4 copy.93
  339.8 0.9 copy.107
  340.7 108.4 %reduce-scatter.4.cloned.1.call-done = bf16[8,1024]{1,0:T(8,128)(2,1)} async-done(((bf16[256,1024]{1,0:T(8,128)(2,1)}), bf16[8,1024]{1,0:T(8,128)(2,1)}) %reduce-scatter.4.cloned.1.call-update) | async-done | bytes 16400
  449.1 0.7 reshape.281
  449.9 33.7 %psum.8 = bf16[4,8,256]{2,1,0:T(8,128)(2,1)S(1)} all-reduce(bf16[4,8,256]{2,1,0:T(8,128)(2,1)S(1)} %copy.94), channel_id=1, replica_groups=mesh['cell'=32,'brick'=8] {'brick'}, use_global_device_ids=true, to_apply=%region_8.9 | all-reduce | flops 8192 | bytes 32768 | tf_op jit(solution)/shard_map/psum | solution.py:192
  483.6 0.6 add_divide_fusion.1
  (48 shorter events, 1.7 us)
Async XLA Ops:
  7.2 1.6 copy-start
  56.4 13.4 %all-to-all-start = ((bf16[2,8,32,256]{3,2,0,1:T(8,128)(2,1)}), bf16[2,8,32,256]{3,2,0,1:T(8,128)(2,1)S(1)}, u32[]{:S(2)}, u32[]{:S(2)}) async-start(bf16[2,8,32,256]{3,2,0,1:T(8,128)(2,1)} %copy.53), calls=%async_computation | async-start | bytes 524288 | tf_op jit(solution)/shard_map/all_to_all | solution.py:153
  154.1 5.6 %copy-start.2 = (bf16[32,8,64,128]{3,2,1,0:T(8,128)(2,1)S(1)}, bf16[32,8,64,128]{3,2,1,0:T(8,128)(2,1)}, u32[]{:S(2)}) copy-start(bf16[32,8,64,128]{3,2,1,0:T(8,128)(2,1)} %copy.103) | copy-start | bytes 12582916
  154.2 6.7 %copy-start.6 = (f32[8]{0:T(128)S(1)}, f32[8]{0:T(128)}, u32[]{:S(2)}) copy-start(f32[8]{0:T(128)} %param.21) | copy-start | bytes 100
  154.2 11.8 %copy-start.5 = (f32[256]{0:T(256)S(1)}, f32[256]{0:T(256)}, u32[]{:S(2)}) copy-start(f32[256]{0:T(256)} %param.23) | copy-start | bytes 3076
  154.2 12.1 %copy-start.7 = (f32[1,1,128]{2,1,0:T(1,128)S(1)}, f32[1,1,128]{2,1,0:T(1,128)}, u32[]{:S(2)}) copy-start(f32[1,1,128]{2,1,0:T(1,128)} %param.24) | copy-start | bytes 1540
  166.3 27.5 %copy-start.8 = (f32[128]{0:T(128)}, f32[128]{0:T(128)S(1)}, u32[]{:S(2)}) copy-start(f32[128]{0:T(128)S(1)} %get-tuple-element.78) | copy-start | bytes 1540
  313.9 170.4 %copy-start.1 = (bf16[4,256]{1,0:T(4,128)(2,1)S(1)}, bf16[4,256]{1,0:T(4,128)(2,1)}, u32[]{:S(2)}) copy-start(bf16[4,256]{1,0:T(4,128)(2,1)} %param.16) | copy-start | bytes 6148
  313.9 169.7 %copy-start.3 = (f32[4,8,256]{2,1,0:T(8,128)S(1)}, f32[4,8,256]{2,1,0:T(8,128)}, u32[]{:S(2)}) copy-start(f32[4,8,256]{2,1,0:T(8,128)} %param.27) | copy-start | bytes 98308
  313.9 169.7 %copy-start.4 = (f32[4,8,256]{2,1,0:T(8,128)S(1)}, f32[4,8,256]{2,1,0:T(8,128)}, u32[]{:S(2)}) copy-start(f32[4,8,256]{2,1,0:T(8,128)} %param.26) | copy-start | bytes 98308
  318.9 10.3 %all-to-all-start.1 = ((bf16[2,8,32,256]{3,2,0,1:T(8,128)(2,1)}), bf16[2,8,32,256]{3,2,0,1:T(8,128)(2,1)S(1)}, u32[]{:S(2)}, u32[]{:S(2)}) async-start(bf16[2,8,32,256]{3,2,0,1:T(8,128)(2,1)} %pad_maximum_fusion.2), calls=%async_computation.1 | async-start | bytes 524288 | tf_op jit(solution)/shard_map/all_to_all | solution.py:174
  322.3 126.8 %reduce-scatter.4.cloned.1.call-start = ((), (), s32[]{:S(2)}) async-start(), calls=%async_computation.3 | async-start | bytes 540672
Sparse Core Ops, SparseCore 0:
  340.8 108.2 reduce-scatter.3
where the time goes:
time: 496 us; the launch traced here: 491 us
  local copies, waits for them, and re-layouts  147 us (30%)
  other arithmetic  120 us (24%)
  waiting for transfers between devices  120 us (24%)
  blocking collectives  77.1 us (16%)
  between operations  14.7 us (3%)
  starting transfers between devices  9.37 us (2%)
    unnamed x2, waiting for transfers between devices  108 us
    unnamed x26, local copies, waits for them, and re-layouts  46.4 us
    scatter-add x1, other arithmetic, tile_step(): key_grads.at[flattened_rows].add(key_edge.reshape(-1, model_width))  44.9 us
    scatter-add x1, other arithmetic, tile_step(): value_grads.at[flattened_rows].add(value_edge.reshape(-1, model_width))  44.7 us
    all_gather x1, blocking collectives, body(): lax.all_gather(master.astype(jnp.bfloat16), 'cell', axis=1, tiled=True)  43.4 us
    gather x2, local copies, waits for them, and re-layouts, tile_step(): value_table[neighbour_rows].reshape(slot_count, TILE, head_count, head_size)  39.7 us
    gather x2, local copies, waits for them, and re-layouts, tile_step(): key_table[neighbour_rows].reshape(slot_count, TILE, head_count, head_size)  39.3 us
    psum x1, blocking collectives, body(): summed = lax.psum(grads.astype(jnp.bfloat16), 'brick')  33.7 us
  transfers between devices with their start and end apart: 3, of which 3 were waited for; matrix products, arithmetic and copies ran while one was open for 1% of the time, Pallas kernels for 0%

commit v1 on v0

v1 whole, which is shorter than its diff:
```python
import functools
import math

import jax
import jax.numpy as jnp
from jax import lax
from jax.experimental import pallas as pl
from jax.experimental.pallas import tpu as pltpu
from jax.sharding import PartitionSpec as P

MESH = pl.DeviceIdType.MESH
loss_weight = 0.0625
epsilon_norm = 1e-06
C = 256
H = 8
A = 128
K = 64
T = 384
CELLS = 32
BRICKS = 8
f32 = jnp.float32
bf16 = jnp.bfloat16


def dot(a, b, dims):
    return lax.dot_general(a, b, (dims, ((), ())), preferred_element_type=f32)


NN = ((1,), (0,))
NT = ((1,), (1,))
TN = ((0,), (0,))


def spread_kernel(feat, spec, table, sends, gain, master, emb, nt, wg, parcel, ssem, rsem, fsem, gsem):
    c = lax.axis_index("cell")
    b = lax.axis_index("brick")
    partner = c + 1 - 2 * lax.rem(c, 2)
    barrier = pltpu.get_barrier_semaphore()
    for k in range(1, 16):
        pl.semaphore_signal(barrier, inc=1, device_id={"cell": lax.rem(c + 2 * k, CELLS), "brick": b}, device_id_type=MESH)
    pl.semaphore_signal(barrier, inc=1, device_id={"cell": partner, "brick": b}, device_id_type=MESH)
    for d in range(1, 8):
        pl.semaphore_signal(barrier, inc=1, device_id={"cell": c, "brick": lax.rem(b + d, BRICKS)}, device_id_type=MESH)
    wg[c] = master[...].reshape(32, C).astype(bf16)

    eye = lax.broadcasted_iota(jnp.int32, (A, A), 0) == lax.broadcasted_iota(jnp.int32, (A, A), 1)
    col = jnp.sum(jnp.where(eye, jnp.broadcast_to(spec[...], (A, A)), 0).astype(f32), axis=1, keepdims=True)
    e = feat[...].astype(f32)
    tab = table[...].astype(f32)
    add = jnp.zeros((A, C), f32)
    for s in range(4):
        add = jnp.where(col == float(s), tab[s : s + 1, :], add)
    e = e + add
    emb[...] = e
    scale = lax.rsqrt(jnp.sum(e * e, axis=1, keepdims=True) * (1.0 / C) + epsilon_norm)
    n = (e * scale * gain[...]).astype(bf16)
    nt[0:A, :] = n
    row_id = lax.broadcasted_iota(jnp.int32, (A, 32), 0)
    for d in range(BRICKS):
        pick = (row_id == sends[d : d + 1, :]).astype(f32).astype(bf16)
        parcel[d] = dot(pick, n, TN).astype(bf16)
    nt[pl.ds(pl.multiple_of(A + 32 * b, 32), 32), :] = parcel[b]
    pl.semaphore_wait(barrier, 23)

    copies = []
    for k in range(1, 16):
        cp = pltpu.make_async_remote_copy(
            src_ref=wg.at[c], dst_ref=wg.at[c], send_sem=ssem.at[k], recv_sem=rsem.at[k],
            device_id={"cell": lax.rem(c + 2 * k, CELLS), "brick": b}, device_id_type=MESH)
        cp.start()
        copies.append(cp)
    ghosts = []
    for d in range(1, 8):
        cp = pltpu.make_async_remote_copy(
            src_ref=parcel.at[lax.rem(b + d, BRICKS)],
            dst_ref=nt.at[pl.ds(pl.multiple_of(A + 32 * b, 32), 32), :],
            send_sem=gsem.at[0, d], recv_sem=gsem.at[1, d],
            device_id={"cell": c, "brick": lax.rem(b + d, BRICKS)}, device_id_type=MESH)
        cp.start()
        ghosts.append(cp)
    forwards = []
    for k in range(16):
        if k:
            copies[k - 1].wait_recv()
        owner = lax.rem(c - 2 * k + CELLS, CELLS)
        cp = pltpu.make_async_remote_copy(
            src_ref=wg.at[owner], dst_ref=wg.at[owner], send_sem=fsem.at[0, k], recv_sem=fsem.at[1, k],
            device_id={"cell": partner, "brick": b}, device_id_type=MESH)
        cp.start()
        forwards.append(cp)
    for cp in ghosts:
        cp.wait()
    for cp in copies:
        cp.wait_send()
    for cp in forwards:
        cp.wait()


def spread(feat, spec, table, sends, gain, master):
    vm = pl.BlockSpec(memory_space=pltpu.VMEM)
    return pl.pallas_call(
        spread_kernel,
        out_shape=(
            jax.ShapeDtypeStruct((A, C), f32),
            jax.ShapeDtypeStruct((T, C), bf16),
            jax.ShapeDtypeStruct((CELLS, 32, C), bf16),
        ),
        in_specs=[vm] * 6,
        out_specs=(vm, vm, vm),
        scratch_shapes=[
            pltpu.VMEM((BRICKS, 32, C), bf16),
            pltpu.SemaphoreType.DMA((16,)),
            pltpu.SemaphoreType.DMA((16,)),
            pltpu.SemaphoreType.DMA((2, 16)),
            pltpu.SemaphoreType.DMA((2, 8)),
        ],
        compiler_params=pltpu.CompilerParams(collective_id=0, has_side_effects=True),
        name="spread",
    )(feat, spec, table, sends, gain, master)


def split(x):
    hi = x.astype(bf16)
    return hi, (x - hi.astype(f32)).astype(bf16)


def attend_kernel(emb, nt, wg, nbr, cnt, dist, decay, readout, target,
                  energy, grads,
                  idx, dst8, rep, qm, gm, big, att, lmat, onehot, pt_hi, pt_lo, idx2):
    scale = 1.0 / math.sqrt(C // H)

    def weight(m):
        return wg[:, 8 * m : 8 * m + 8, :].astype(f32).reshape(C, C).astype(bf16)

    w_q, w_k, w_v, w_o = weight(0), weight(1), weight(2), weight(3)
    n_all = nt[...]
    n_own = nt[0:A, :]
    q = dot(n_own, w_q, NN).astype(bf16)
    k = dot(n_all, w_k, NN).astype(bf16)
    v = dot(n_all, w_v, NN).astype(bf16)

    slot = lax.broadcasted_iota(jnp.int32, (K, A), 0)
    masked = jnp.where(slot < cnt[...], nbr[...], 512)
    m_t = masked.T
    d_t = dist[...].T
    m2 = jnp.concatenate([m_t, m_t], axis=1)
    d2 = jnp.concatenate([d_t, d_t], axis=1)
    idx2[...] = m2
    q32 = q.astype(f32)
    for h in range(H):
        idx[pl.ds(h, A, stride=8), :] = m2
        dst8[pl.ds(h, A, stride=8), :] = d2
        rep[pl.ds(h, A, stride=8), :] = q32[:, 0:128]
        rep[pl.ds(A * H + h, A, stride=8), :] = q32[:, 128:256]

    rows = A * H
    head_of_lane = lax.broadcasted_iota(jnp.int32, (rows, C), 1) // 32
    head_of_row = lax.rem(lax.broadcasted_iota(jnp.int32, (rows, C), 0), 8)
    head_mask = head_of_lane == head_of_row

    def spread_heads():
        x = jnp.concatenate([rep[0:rows, :], rep[rows : 2 * rows, :]], axis=1)
        return jnp.where(head_mask, x, 0.0).astype(bf16)

    qm[...] = spread_heads()
    big[...] = dot(qm[...], k, NT)

    lane = lax.broadcasted_iota(jnp.int32, (A, 128), 1)
    row_in = lax.broadcasted_iota(jnp.int32, (A, 128), 0)
    sub_head = lax.rem(row_in, 8)
    dec = jnp.zeros((A, 128), f32)
    for h in range(H):
        dec = jnp.where(sub_head == h, decay[h], dec)
    diag = lax.rem(row_in // 8, 2) == lane // 64
    t_row = lax.broadcasted_iota(jnp.int32, (T, 128), 0)
    lmat[...] = jnp.zeros((128, 1024), bf16)
    lane8 = lax.broadcasted_iota(jnp.int32, (8, 128), 1)

    def pick(s):
        r0 = pl.multiple_of(s * 128, 128)
        ix = idx[pl.ds(r0, 128), :]
        low = jnp.bitwise_and(ix, 127)
        blk = ix // 128
        out = jnp.zeros((128, 128), f32)
        for t in range(3):
            g = jnp.take_along_axis(big[pl.ds(r0, 128), 128 * t : 128 * t + 128], low, axis=1)
            out = jnp.where(blk == t, g, out)
        return out, ix < 512

    def scatter(s, w16):
        w32 = jnp.where(diag, w16.astype(f32), 0.0).astype(bf16)
        for t in range(8):
            lmat[16 * t : 16 * t + 16, 128 * t : 128 * t + 128] = w32[16 * t : 16 * t + 16, :]
        p = dot(onehot[s], lmat[...], NT)
        hi, lo = split(p)
        c0 = pl.multiple_of(s * 128, 128)
        pt_hi[:, pl.ds(c0, 128)] = hi
        pt_lo[:, pl.ds(c0, 128)] = lo

    @pl.loop(0, 8)
    def _(s):
        ev = idx2[pl.ds(16 * s, 8, stride=2), :]
        od = idx2[pl.ds(16 * s + 1, 8, stride=2), :]
        pair = jnp.where(lane8 < 64, ev, od)
        for t in range(8):
            hit = t_row == pair[t : t + 1, :]
            onehot[s, :, 128 * t : 128 * t + 128] = jnp.where(hit, 1.0, 0.0).astype(bf16)

    @pl.loop(0, 8)
    def _(s):
        r0 = pl.multiple_of(s * 128, 128)
        got, ok = pick(s)
        score = got * scale - dec * dst8[pl.ds(r0, 128), :]
        score = jnp.where(ok, score, -1e30)
        top = jnp.max(score, axis=1, keepdims=True)
        ex = jnp.where(ok, jnp.exp(score - top), 0.0)
        a = ex / (jnp.sum(ex, axis=1, keepdims=True) * 0.5)
        att[pl.ds(r0, 128), :] = a
        scatter(s, a.astype(bf16))

    lane_r = lax.broadcasted_iota(jnp.int32, (C, rows), 1)
    head_sel = lax.rem(lane_r, 8) == lax.broadcasted_iota(jnp.int32, (C, rows), 0) // 32
    collect = (lax.broadcasted_iota(jnp.int32, (A, rows), 1) // 8
               == lax.broadcasted_iota(jnp.int32, (A, rows), 0)).astype(f32).astype(bf16)

    def gather_heads(table_t, mult):
        full = dot(table_t, pt_hi[...], NN) + dot(table_t, pt_lo[...], NN)
        if mult is not None:
            full = full * mult
        kept = jnp.where(head_sel, full, 0.0).astype(bf16)
        return dot(collect, kept, NT).astype(bf16)

    attended = gather_heads(v.astype(f32).T.astype(bf16), None)
    updated = emb[...] + dot(attended, w_o, NN)
    sig = jax.nn.sigmoid(updated)
    e_col = jnp.sum(readout[...] * (updated * sig), axis=1, keepdims=True)
    eye = lax.broadcasted_iota(jnp.int32, (A, A), 0) == lax.broadcasted_iota(jnp.int32, (A, A), 1)
    energy[...] = jnp.sum(jnp.where(eye, e_col, 0.0), axis=0, keepdims=True)
    t_col = jnp.sum(jnp.where(eye, target[...], 0.0), axis=1, keepdims=True)
    grad_energy = loss_weight * (e_col - t_col)
    slope = sig * (1.0 + updated * (1.0 - sig))
    grad_updated = (grad_energy * readout[...] * slope).astype(bf16)
    grad_att = dot(grad_updated, w_o, NT).astype(bf16)

    def put(m, x):
        grads[2 * m] = x[:, 0:128].astype(bf16)
        grads[2 * m + 1] = x[:, 128:256].astype(bf16)

    put(3, dot(attended, grad_updated, TN))
    g32 = grad_att.astype(f32)
    for h in range(H):
        rep[pl.ds(h, A, stride=8), :] = g32[:, 0:128]
        rep[pl.ds(A * H + h, A, stride=8), :] = g32[:, 128:256]
    gm[...] = spread_heads()
    big[...] = dot(gm[...], v, NT)

    def table_grad(rows_m, mult):
        tg = dot(pt_hi[...], rows_m, NN) + dot(pt_lo[...], rows_m, NN)
        if mult is not None:
            tg = tg * mult
        hi, lo = split(tg)
        return dot(n_all, hi, TN) + dot(n_all, lo, TN)

    put(2, table_grad(gm[...], None))

    @pl.loop(0, 8)
    def _(s):
        r0 = pl.multiple_of(s * 128, 128)
        gw, ok = pick(s)
        a = att[pl.ds(r0, 128), :]
        mean = jnp.sum(a * gw, axis=1, keepdims=True) * 0.5
        scatter(s, (a * (gw - mean)).astype(bf16))

    grad_query = gather_heads(k.astype(f32).T.astype(bf16), scale)
    put(0, dot(n_own, grad_query, TN))
    put(1, table_grad(qm[...], scale))


def attend(emb, nt, wg, nbr, cnt, dist, decay, readout, target):
    vm = pl.BlockSpec(memory_space=pltpu.VMEM)
    sm = pl.BlockSpec(memory_space=pltpu.SMEM)
    return pl.pallas_call(
        attend_kernel,
        out_shape=(
            jax.ShapeDtypeStruct((1, A), f32),
            jax.ShapeDtypeStruct((8, C, 128), bf16),
        ),
        in_specs=[vm] * 6 + [sm] + [vm] * 2,
        out_specs=(vm, vm),
        scratch_shapes=[
            pltpu.VMEM((A * H, 128), jnp.int32),
            pltpu.VMEM((A * H, 128), f32),
            pltpu.VMEM((2 * A * H, 128), f32),
            pltpu.VMEM((A * H, C), bf16),
            pltpu.VMEM((A * H, C), bf16),
            pltpu.VMEM((A * H, T), f32),
            pltpu.VMEM((A * H, 128), f32),
            pltpu.VMEM((128, 1024), bf16),
            pltpu.VMEM((8, T, 1024), bf16),
            pltpu.VMEM((T, A * H), bf16),
            pltpu.VMEM((T, A * H), bf16),
            pltpu.VMEM((A, 128), jnp.int32),
        ],
        name="attend",
    )(emb, nt, wg, nbr, cnt, dist, decay, readout, target)


def reduce_kernel(g, out, r1, s2, r2, fin, sem1, sem2, sem3):
    c = lax.axis_index("cell")
    b = lax.axis_index("brick")
    barrier = pltpu.get_barrier_semaphore()
    for k in range(1, CELLS):
        pl.semaphore_signal(barrier, inc=1, device_id={"cell": lax.rem(c + k, CELLS), "brick": b}, device_id_type=MESH)
    for d in range(1, BRICKS):
        pl.semaphore_signal(barrier, inc=1, device_id={"cell": c, "brick": lax.rem(b + d, BRICKS)}, device_id_type=MESH)
    pl.semaphore_wait(barrier, CELLS - 1 + BRICKS - 1)

    first = []
    for d in range(1, BRICKS):
        to = lax.rem(b + d, BRICKS)
        cp = pltpu.make_async_remote_copy(
            src_ref=g.at[to], dst_ref=r1.at[b], send_sem=sem1.at[0, d], recv_sem=sem1.at[1, d],
            device_id={"cell": c, "brick": to}, device_id_type=MESH)
        cp.start()
        first.append(cp)
    total = g[b].astype(f32)
    for d in range(1, BRICKS):
        first[d - 1].wait_recv()
        total = total + r1[lax.rem(b - d + BRICKS, BRICKS)].astype(f32)
    s2[...] = total.reshape(CELLS, 8, 128).astype(s2.dtype)

    second = []
    for k in range(1, CELLS):
        to = lax.rem(c + k, CELLS)
        cp = pltpu.make_async_remote_copy(
            src_ref=s2.at[to], dst_ref=r2.at[c], send_sem=sem2.at[0, k], recv_sem=sem2.at[1, k],
            device_id={"cell": to, "brick": b}, device_id_type=MESH)
        cp.start()
        second.append(cp)
    r2[c] = s2[c]
    for cp in second:
        cp.wait_recv()
    fin[b] = jnp.sum(r2[...].astype(f32), axis=0)

    third = []
    for d in range(1, BRICKS):
        cp = pltpu.make_async_remote_copy(
            src_ref=fin.at[b], dst_ref=fin.at[b], send_sem=sem3.at[0, d], recv_sem=sem3.at[1, d],
            device_id={"cell": c, "brick": lax.rem(b + d, BRICKS)}, device_id_type=MESH)
        cp.start()
        third.append(cp)
    for cp in first + second:
        cp.wait_send()
    for cp in third:
        cp.wait()
    for m in range(4):
        out[m] = jnp.concatenate([fin[2 * m], fin[2 * m + 1]], axis=1)


def reduce(g):
    vm = pl.BlockSpec(memory_space=pltpu.VMEM)
    return pl.pallas_call(
        reduce_kernel,
        out_shape=jax.ShapeDtypeStruct((4, 8, C), f32),
        in_specs=[vm],
        out_specs=vm,
        scratch_shapes=[
            pltpu.VMEM((BRICKS, C, 128), bf16),
            pltpu.VMEM((CELLS, 8, 128), f32),
            pltpu.VMEM((CELLS, 8, 128), f32),
            pltpu.VMEM((BRICKS, 8, 128), f32),
            pltpu.SemaphoreType.DMA((2, BRICKS)),
            pltpu.SemaphoreType.DMA((2, CELLS)),
            pltpu.SemaphoreType.DMA((2, BRICKS)),
        ],
        compiler_params=pltpu.CompilerParams(collective_id=1, has_side_effects=True),
        name="reduce",
    )(g)


def body(features, species, species_table, neighbours, counts, send_lists, distances,
         head_decay, norm_gain, readout, targets, master, moment, second):
    emb, nt, wg = spread(
        features.reshape(A, C), species.reshape(1, A), species_table,
        send_lists.reshape(BRICKS, 32), norm_gain.reshape(1, C), master)
    energy, grads = attend(
        emb, nt, wg, neighbours.reshape(K, A), counts.reshape(1, A), distances.reshape(K, A),
        head_decay, readout.reshape(1, C), targets.reshape(1, A))
    owned = reduce(grads)
    moment_new = 0.9 * moment + 0.1 * owned
    second_new = 0.999 * second + 0.001 * owned * owned
    adam_step = moment_new / (jnp.sqrt(second_new) + 1e-08)
    return (energy.reshape(1, 1, A), moment_new, second_new, adam_step)


def solution(mesh):
    return jax.shard_map(
        body,
        mesh=mesh,
        in_specs=(
            P("cell", "brick", None, None),
            P("cell", "brick", None),
            P(),
            P("cell", "brick", None, None),
            P("cell", "brick", None),
            P("cell", "brick", None, None),
            P("cell", "brick", None, None),
            P(),
            P(),
            P(),
            P("cell", "brick", None),
            P(None, "cell", None),
            P(None, "cell", None),
            P(None, "cell", None),
        ),
        out_specs=(
            P("cell", "brick", None),
            P(None, "cell", None),
            P(None, "cell", None),
            P(None, "cell", None),
        ),
        check_vma=False,
    )
```

time: 496 us -> 71.9 us (0.14)
  the two profiles are of different devices: /device:TPU:16 before, /device:TPU:1 now
where the time goes in v1:
time: 71.9 us; the launch traced here: 71.6 us
  Pallas kernels  69.6 us (97%)
  other arithmetic  1.4 us (2%)
    pallas_call x1, Pallas kernels, reduce(): pl.pallas_call(reduce_kernel, out_shape=jax.ShapeDtypeStruct((4, 8, C), f...  26 us
    pallas_call x1, Pallas kernels, spread(): pl.pallas_call(spread_kernel, out_shape=(jax.ShapeDtypeStruct((A, C), f32...  22.7 us
    pallas_call x1, Pallas kernels, attend(): pl.pallas_call(attend_kernel, out_shape=(jax.ShapeDtypeStruct((1, A), f32...  20.8 us

profile of v1, /device:TPU:1, one launch (start us, length us, event | category | flops | bytes accessed | tf_op | source)
XLA Modules:
  0.0 71.6 jit_solution(14383429810206486691)
XLA Ops:
  0.6 22.7 %spread.1 = (f32[128,256]{1,0:T(8,128)}, bf16[384,256]{1,0:T(8,128)(2,1)}, bf16[32,32,256]{2,1,0:T(8,128)(2,1)}) custom-call(bf16[128,256]{1,0:T(8,128)(2,1)} %bitcast.10, s32[1,128]{1,0:T(1,128)} %bitcast.16, bf16[4,256]{1,0:T(4,128)(2,1)} %table.1, s32[8,32]{1,0:T(8,128)} %bitcast.13, f32[1,256]{1,0:T(1,128)} %bitcast.14, f32[4,8,256]{2,1,0:T(8,128)} %master.1), custom_call_target="tpu_custom_call" | custom-call | tf_op jit(solution)/shard_map/spread/pallas_call | solution.py:101
  23.4 20.8 %attend.1 = (f32[1,128]{1,0:T(1,128)}, bf16[8,256,128]{2,1,0:T(8,128)(2,1)}) custom-call(f32[128,256]{1,0:T(8,128)} %get-tuple-element.9.emb, bf16[384,256]{1,0:T(8,128)(2,1)} %get-tuple-element.10.nt, bf16[32,32,256]{2,1,0:T(8,128)(2,1)} %get-tuple-element.11.wg, s32[64,128]{1,0:T(8,128)} %bitcast.11, s32[1,128]{1,0:T(1,128)} %bitcast.17, ...), custom_call_target="tpu_custom_call" | custom-call | tf_op jit(solution)/shard_map/attend/pallas_call | solution.py:282
  44.2 0.0 copy-start
  44.2 0.0 copy-start.1
  44.2 26.0 %reduce.1 = f32[4,8,256]{2,1,0:T(8,128)} custom-call(bf16[8,256,128]{2,1,0:T(8,128)(2,1)} %get-tuple-element.13.g), custom_call_target="tpu_custom_call" | custom-call | tf_op jit(solution)/shard_map/reduce/pallas_call | solution.py:362
  70.2 0.0 copy-done
  70.2 0.0 copy-done.1
  70.2 1.4 %add_divide_fusion = (f32[4,8,256]{2,1,0:T(8,128)}, f32[4,8,256]{2,1,0:T(8,128)}, f32[4,8,256]{2,1,0:T(8,128)}) fusion(f32[4,8,256]{2,1,0:T(8,128)} %reduce.1, f32[4,8,256]{2,1,0:T(8,128)S(1)} %copy-done, f32[4,8,256]{2,1,0:T(8,128)S(1)} %copy-done.1), kind=kLoop, calls=%fused_computation.2 | loop fusion | flops 73728 | bytes 196608 | tf_op jit(solution)/shard_map/div | solution.py:392
Async XLA Ops:
  44.2 26.1 %copy-start = (f32[4,8,256]{2,1,0:T(8,128)S(1)}, f32[4,8,256]{2,1,0:T(8,128)}, u32[]{:S(2)}) copy-start(f32[4,8,256]{2,1,0:T(8,128)} %param.27) | copy-start | bytes 98308
  44.2 26.1 %copy-start.1 = (f32[4,8,256]{2,1,0:T(8,128)S(1)}, f32[4,8,256]{2,1,0:T(8,128)}, u32[]{:S(2)}) copy-start(f32[4,8,256]{2,1,0:T(8,128)} %param.26) | copy-start | bytes 98308

commit v2 on v1

v2 whole, which is shorter than its diff:
```python
import functools
import math

import jax
import jax.numpy as jnp
from jax import lax
from jax.experimental import pallas as pl
from jax.experimental.pallas import tpu as pltpu
from jax.sharding import PartitionSpec as P

MESH = pl.DeviceIdType.MESH
loss_weight = 0.0625
epsilon_norm = 1e-06
C = 256
H = 8
A = 128
K = 64
T = 384
CELLS = 32
BRICKS = 8
f32 = jnp.float32
bf16 = jnp.bfloat16


def dot(a, b, dims):
    return lax.dot_general(a, b, (dims, ((), ())), preferred_element_type=f32)


NN = ((1,), (0,))
NT = ((1,), (1,))
TN = ((0,), (0,))


def split(x):
    hi = x.astype(bf16)
    return hi, (x - hi.astype(f32)).astype(bf16)


def peer(cell, brick):
    return {"cell": cell, "brick": brick}


def step_kernel(feat, spec, table, sends, gain, master, nbr, cnt, dist, decay, readout, target,
                energy, out,
                emb, nt, wa, wb, parcel,
                idx, dst8, rep, qm, gm, big, att, lmat, onehot, pt_hi, pt_lo, idx2,
                gtmp, gsend, r1, s2f, s2, r2, fin,
                sem_a, sem_b, sem_g, sem_1, sem_2, sem_3):
    c = lax.axis_index("cell")
    b = lax.axis_index("brick")
    partner = c + 1 - 2 * lax.rem(c, 2)
    barrier = pltpu.get_barrier_semaphore()
    for k in range(1, CELLS):
        pl.semaphore_signal(barrier, inc=1, device_id=peer(lax.rem(c + k, CELLS), b), device_id_type=MESH)
    for d in range(1, BRICKS):
        pl.semaphore_signal(barrier, inc=1, device_id=peer(c, lax.rem(b + d, BRICKS)), device_id_type=MESH)

    wa[c] = master[0:2].reshape(16, C).astype(bf16)
    wb[c] = master[2:4].reshape(16, C).astype(bf16)
    eye = lax.broadcasted_iota(jnp.int32, (A, A), 0) == lax.broadcasted_iota(jnp.int32, (A, A), 1)
    col = jnp.sum(jnp.where(eye, jnp.broadcast_to(spec[...], (A, A)), 0).astype(f32), axis=1, keepdims=True)
    e = feat[...].astype(f32)
    tab = table[...].astype(f32)
    add = jnp.zeros((A, C), f32)
    for s in range(4):
        add = jnp.where(col == float(s), tab[s : s + 1, :], add)
    e = e + add
    emb[...] = e
    rms = lax.rsqrt(jnp.sum(e * e, axis=1, keepdims=True) * (1.0 / C) + epsilon_norm)
    n = (e * rms * gain[...]).astype(bf16)
    nt[0:A, :] = n
    row_id = lax.broadcasted_iota(jnp.int32, (A, 32), 0)
    for d in range(BRICKS):
        take = (row_id == sends[d : d + 1, :]).astype(f32).astype(bf16)
        parcel[d] = dot(take, n, TN).astype(bf16)
    nt[pl.ds(pl.multiple_of(A + 32 * b, 32), 32), :] = parcel[b]
    pl.semaphore_wait(barrier, CELLS - 1 + BRICKS - 1)

    def same_core(w, sem):
        made = []
        for k in range(1, 16):
            cp = pltpu.make_async_remote_copy(
                src_ref=w.at[c], dst_ref=w.at[c], send_sem=sem.at[0, k], recv_sem=sem.at[1, k],
                device_id=peer(lax.rem(c + 2 * k, CELLS), b), device_id_type=MESH)
            cp.start()
            made.append(cp)
        return made

    def forward(w, sem, made):
        sent = []
        for k in range(16):
            if k:
                made[k - 1].wait_recv()
            owner = lax.rem(c - 2 * k + CELLS, CELLS)
            cp = pltpu.make_async_remote_copy(
                src_ref=w.at[owner], dst_ref=w.at[owner], send_sem=sem.at[2, k], recv_sem=sem.at[3, k],
                device_id=peer(partner, b), device_id_type=MESH)
            cp.start()
            sent.append(cp)
        return sent

    made_a = same_core(wa, sem_a)
    ghosts = []
    for d in range(1, BRICKS):
        to = lax.rem(b + d, BRICKS)
        cp = pltpu.make_async_remote_copy(
            src_ref=parcel.at[to],
            dst_ref=nt.at[pl.ds(pl.multiple_of(A + 32 * b, 32), 32), :],
            send_sem=sem_g.at[0, d], recv_sem=sem_g.at[1, d],
            device_id=peer(c, to), device_id_type=MESH)
        cp.start()
        ghosts.append(cp)
    made_b = same_core(wb, sem_b)

    scale = 1.0 / math.sqrt(C // H)
    rows = A * H
    slot = lax.broadcasted_iota(jnp.int32, (K, A), 0)
    masked = jnp.where(slot < cnt[...], nbr[...], 512)
    m_t = masked.T
    d_t = dist[...].T
    m2 = jnp.concatenate([m_t, m_t], axis=1)
    d2 = jnp.concatenate([d_t, d_t], axis=1)
    idx2[...] = m2
    for h in range(H):
        idx[pl.ds(h, A, stride=8), :] = m2
        dst8[pl.ds(h, A, stride=8), :] = d2
    lmat[...] = jnp.zeros((128, 1024), bf16)
    t_row = lax.broadcasted_iota(jnp.int32, (T, 128), 0)
    lane8 = lax.broadcasted_iota(jnp.int32, (8, 128), 1)

    @pl.loop(0, 8)
    def _(s):
        ev = idx2[pl.ds(16 * s, 8, stride=2), :]
        od = idx2[pl.ds(16 * s + 1, 8, stride=2), :]
        pair = jnp.where(lane8 < 64, ev, od)
        for t in range(8):
            hit = t_row == pair[t : t + 1, :]
            onehot[s, :, 128 * t : 128 * t + 128] = jnp.where(hit, 1.0, 0.0).astype(bf16)

    sent_a = forward(wa, sem_a, made_a)
    for cp in ghosts:
        cp.wait()
    for cp in sent_a:
        cp.wait_recv()

    def weight(w, m):
        return w[:, 8 * m : 8 * m + 8, :].astype(f32).reshape(C, C).astype(bf16)

    n_all = nt[...]
    n_own = nt[0:A, :]
    q = dot(n_own, weight(wa, 0), NN).astype(bf16)
    k = dot(n_all, weight(wa, 1), NN).astype(bf16)

    head_of_lane = lax.broadcasted_iota(jnp.int32, (rows, C), 1) // 32
    head_of_row = lax.rem(lax.broadcasted_iota(jnp.int32, (rows, C), 0), 8)
    head_mask = head_of_lane == head_of_row

    def spread_heads(x32):
        for h in range(H):
            rep[pl.ds(h, A, stride=8), :] = x32[:, 0:128]
            rep[pl.ds(rows + h, A, stride=8), :] = x32[:, 128:256]
        x = jnp.concatenate([rep[0:rows, :], rep[rows : 2 * rows, :]], axis=1)
        return jnp.where(head_mask, x, 0.0).astype(bf16)

    qm[...] = spread_heads(q.astype(f32))
    big[...] = dot(qm[...], k, NT)
    sent_b = forward(wb, sem_b, made_b)

    lane = lax.broadcasted_iota(jnp.int32, (128, 128), 1)
    row_in = lax.broadcasted_iota(jnp.int32, (128, 128), 0)
    sub_head = lax.rem(row_in, 8)
    dec = jnp.zeros((128, 128), f32)
    for h in range(H):
        dec = jnp.where(sub_head == h, decay[h], dec)
    diag = lax.rem(row_in // 8, 2) == lane // 64

    def pick(s):
        r0 = pl.multiple_of(s * 128, 128)
        ix = idx[pl.ds(r0, 128), :]
        low = jnp.bitwise_and(ix, 127)
        res = jnp.zeros((128, 128), f32)
        for t in range(3):
            g = jnp.take_along_axis(big[pl.ds(r0, 128), 128 * t : 128 * t + 128], low, axis=1)
            res = jnp.where(ix >= 128 * t, g, res)
        return res, ix < 512

    def scatter(s, w32):
        kept = jnp.where(diag, w32, 0.0).astype(bf16)
        for t in range(8):
            lmat[16 * t : 16 * t + 16, 128 * t : 128 * t + 128] = kept[16 * t : 16 * t + 16, :]
        hi, lo = split(dot(onehot[s], lmat[...], NT))
        c0 = pl.multiple_of(s * 128, 128)
        pt_hi[:, pl.ds(c0, 128)] = hi
        pt_lo[:, pl.ds(c0, 128)] = lo

    @pl.loop(0, 8)
    def _(s):
        r0 = pl.multiple_of(s * 128, 128)
        got, ok = pick(s)
        score = got * scale - dec * dst8[pl.ds(r0, 128), :]
        score = jnp.where(ok, score, -1e30)
        top = jnp.max(score, axis=1, keepdims=True)
        ex = jnp.where(ok, jnp.exp(score - top), 0.0)
        a = ex / (jnp.sum(ex, axis=1, keepdims=True) * 0.5)
        att[pl.ds(r0, 128), :] = a
        scatter(s, a)

    for cp in sent_b:
        cp.wait_recv()
    w_o = weight(wb, 1)
    v = dot(n_all, weight(wb, 0), NN).astype(bf16)

    head_sel = (lax.rem(lax.broadcasted_iota(jnp.int32, (C, rows), 1), 8)
                == lax.broadcasted_iota(jnp.int32, (C, rows), 0) // 32)
    collect = (lax.broadcasted_iota(jnp.int32, (A, rows), 1) // 8
               == lax.broadcasted_iota(jnp.int32, (A, rows), 0)).astype(f32).astype(bf16)

    def gather_heads(table_t, mult):
        full = dot(table_t, pt_hi[...], NN) + dot(table_t, pt_lo[...], NN)
        if mult is not None:
            full = full * mult
        kept = jnp.where(head_sel, full, 0.0).astype(bf16)
        return dot(collect, kept, NT).astype(bf16)

    attended = gather_heads(v.astype(f32).T.astype(bf16), None)
    updated = emb[...] + dot(attended, w_o, NN)
    sig = jax.nn.sigmoid(updated)
    e_col = jnp.sum(readout[...] * (updated * sig), axis=1, keepdims=True)
    energy[...] = jnp.sum(jnp.where(eye, e_col, 0.0), axis=0, keepdims=True)
    t_col = jnp.sum(jnp.where(eye, target[...], 0.0), axis=1, keepdims=True)
    grad_energy = loss_weight * (e_col - t_col)
    slope = sig * (1.0 + updated * (1.0 - sig))
    grad_updated = (grad_energy * readout[...] * slope).astype(bf16)
    grad_att = dot(grad_updated, w_o, NT).astype(bf16)

    first = [None] * 4

    def put(m, x):
        gtmp[0:C, :] = x[:, 0:128]
        gtmp[C : 2 * C, :] = x[:, 128:256]
        for d in range(BRICKS):
            gsend[m, d] = jnp.concatenate(
                [gtmp[pl.ds(d, CELLS, stride=8), :], gtmp[pl.ds(C + d, CELLS, stride=8), :]], axis=1).astype(bf16)
        made = []
        for d in range(1, BRICKS):
            to = lax.rem(b + d, BRICKS)
            cp = pltpu.make_async_remote_copy(
                src_ref=gsend.at[m, to], dst_ref=r1.at[m, b], send_sem=sem_1.at[m, 0, d], recv_sem=sem_1.at[m, 1, d],
                device_id=peer(c, to), device_id_type=MESH)
            cp.start()
            made.append(cp)
        first[m] = made

    put(3, dot(attended, grad_updated, TN))
    gm[...] = spread_heads(grad_att.astype(f32))
    big[...] = dot(gm[...], v, NT)

    def table_grad(rows_m, mult):
        tg = dot(pt_hi[...], rows_m, NN) + dot(pt_lo[...], rows_m, NN)
        if mult is not None:
            tg = tg * mult
        hi, lo = split(tg)
        return dot(n_all, hi, TN) + dot(n_all, lo, TN)

    put(2, table_grad(gm[...], None))

    @pl.loop(0, 8)
    def _(s):
        r0 = pl.multiple_of(s * 128, 128)
        gw, ok = pick(s)
        a = att[pl.ds(r0, 128), :]
        mean = jnp.sum(a * gw, axis=1, keepdims=True) * 0.5
        scatter(s, a * (gw - mean))

    put(1, table_grad(qm[...], scale))
    grad_query = gather_heads(k.astype(f32).T.astype(bf16), scale)
    put(0, dot(n_own, grad_query, TN))

    for m in (3, 2, 1, 0):
        total = gsend[m, b].astype(f32)
        for d in range(1, BRICKS):
            first[m][d - 1].wait_recv()
            total = total + r1[m, lax.rem(b - d + BRICKS, BRICKS)].astype(f32)
        s2f[pl.ds(2 * m, CELLS, stride=8), :] = total[:, 0:128]
        s2f[pl.ds(2 * m + 1, CELLS, stride=8), :] = total[:, 128:256]
    s2[...] = s2f[...].reshape(CELLS, 8, 128).astype(bf16)

    second = []
    for k in range(1, CELLS):
        to = lax.rem(c + k, CELLS)
        cp = pltpu.make_async_remote_copy(
            src_ref=s2.at[to], dst_ref=r2.at[c], send_sem=sem_2.at[0, k], recv_sem=sem_2.at[1, k],
            device_id=peer(to, b), device_id_type=MESH)
        cp.start()
        second.append(cp)
    r2[c] = s2[c]
    for cp in made_a + made_b + sent_a + sent_b:
        cp.wait_send()
    for m in range(4):
        for cp in first[m]:
            cp.wait_send()
    for cp in second:
        cp.wait_recv()
    mine = pl.ds(pl.multiple_of(8 * b, 8), 8)
    fin[mine, :] = jnp.sum(r2[...].astype(f32), axis=0)

    third = []
    for d in range(1, BRICKS):
        cp = pltpu.make_async_remote_copy(
            src_ref=fin.at[mine, :], dst_ref=fin.at[mine, :], send_sem=sem_3.at[0, d], recv_sem=sem_3.at[1, d],
            device_id=peer(c, lax.rem(b + d, BRICKS)), device_id_type=MESH)
        cp.start()
        third.append(cp)
    for cp in second:
        cp.wait_send()
    for cp in third:
        cp.wait()
    for m in range(4):
        out[m] = jnp.concatenate([fin[pl.ds(2 * m, 8, stride=8), :], fin[pl.ds(2 * m + 1, 8, stride=8), :]], axis=1)


def step(*args):
    vm = pl.BlockSpec(memory_space=pltpu.VMEM)
    sm = pl.BlockSpec(memory_space=pltpu.SMEM)
    rows = A * H
    dma = pltpu.SemaphoreType.DMA
    return pl.pallas_call(
        step_kernel,
        out_shape=(jax.ShapeDtypeStruct((1, A), f32), jax.ShapeDtypeStruct((4, 8, C), f32)),
        in_specs=[vm] * 9 + [sm] + [vm] * 2,
        out_specs=(vm, vm),
        scratch_shapes=[
            pltpu.VMEM((A, C), f32),
            pltpu.VMEM((T, C), bf16),
            pltpu.VMEM((CELLS, 16, C), bf16),
            pltpu.VMEM((CELLS, 16, C), bf16),
            pltpu.VMEM((BRICKS, 32, C), bf16),
            pltpu.VMEM((rows, 128), jnp.int32),
            pltpu.VMEM((rows, 128), f32),
            pltpu.VMEM((2 * rows, 128), f32),
            pltpu.VMEM((rows, C), bf16),
            pltpu.VMEM((rows, C), bf16),
            pltpu.VMEM((rows, T), f32),
            pltpu.VMEM((rows, 128), f32),
            pltpu.VMEM((128, 1024), bf16),
            pltpu.VMEM((8, T, 1024), bf16),
            pltpu.VMEM((T, rows), bf16),
            pltpu.VMEM((T, rows), bf16),
            pltpu.VMEM((A, 128), jnp.int32),
            pltpu.VMEM((2 * C, 128), f32),
            pltpu.VMEM((4, BRICKS, CELLS, C), bf16),
            pltpu.VMEM((4, BRICKS, CELLS, C), bf16),
            pltpu.VMEM((CELLS * 8, 128), f32),
            pltpu.VMEM((CELLS, 8, 128), bf16),
            pltpu.VMEM((CELLS, 8, 128), bf16),
            pltpu.VMEM((BRICKS * 8, 128), f32),
            dma((4, 16)),
            dma((4, 16)),
            dma((2, BRICKS)),
            dma((4, 2, BRICKS)),
            dma((2, CELLS)),
            dma((2, BRICKS)),
        ],
        compiler_params=pltpu.CompilerParams(collective_id=0, has_side_effects=True),
        name="step",
    )(*args)


def body(features, species, species_table, neighbours, counts, send_lists, distances,
         head_decay, norm_gain, readout, targets, master, moment, second):
    energy, owned = step(
        features.reshape(A, C), species.reshape(1, A), species_table,
        send_lists.reshape(BRICKS, 32), norm_gain.reshape(1, C), master,
        neighbours.reshape(K, A), counts.reshape(1, A), distances.reshape(K, A),
        head_decay, readout.reshape(1, C), targets.reshape(1, A))
    moment_new = 0.9 * moment + 0.1 * owned
    second_new = 0.999 * second + 0.001 * owned * owned
    adam_step = moment_new / (jnp.sqrt(second_new) + 1e-08)
    return (energy.reshape(1, 1, A), moment_new, second_new, adam_step)


def solution(mesh):
    return jax.shard_map(
        body,
        mesh=mesh,
        in_specs=(
            P("cell", "brick", None, None),
            P("cell", "brick", None),
            P(),
            P("cell", "brick", None, None),
            P("cell", "brick", None),
            P("cell", "brick", None, None),
            P("cell", "brick", None, None),
            P(),
            P(),
            P(),
            P("cell", "brick", None),
            P(None, "cell", None),
            P(None, "cell", None),
            P(None, "cell", None),
        ),
        out_specs=(
            P("cell", "brick", None),
            P(None, "cell", None),
            P(None, "cell", None),
            P(None, "cell", None),
        ),
        check_vma=False,
    )
```

time: 71.9 us -> 60.5 us (0.84)
  Pallas kernels: 69.6 us -> 57 us
  local copies, waits for them, and re-layouts: 0.01 us -> 1.2 us
    pallas_call x3 -> x1, Pallas kernels: 69.6 us -> 57 us  [step(): pl.pallas_call(step_kernel, out_shape=(jax.ShapeDtypeStruct((1, A), f32),...]
    unnamed x4 -> x7, local copies, waits for them, and re-layouts: 0.01 us -> 1.2 us
where the time goes in v2:
time: 60.5 us; the launch traced here: 60.3 us
  Pallas kernels  57 us (94%)
  other arithmetic  1.4 us (2%)
  local copies, waits for them, and re-layouts  1.2 us (2%)
  between operations  0.68 us (1%)
    pallas_call x1, Pallas kernels, step(): pl.pallas_call(step_kernel, out_shape=(jax.ShapeDtypeStruct((1, A), f32),...  57 us
    div x1, other arithmetic, body(): adam_step = moment_new / (jnp.sqrt(second_new) + 1e-08)  1.4 us

profile of v2, /device:TPU:1, one launch (start us, length us, event | category | flops | bytes accessed | tf_op | source)
XLA Modules:
  0.0 60.3 jit_solution(10487377497559624151)
XLA Ops:
  0.6 0.0 copy-start
  0.6 0.0 copy-start.1
  0.7 57.0 %step.1 = (f32[1,128]{1,0:T(1,128)}, f32[4,8,256]{2,1,0:T(8,128)}) custom-call(bf16[128,256]{1,0:T(8,128)(2,1)} %bitcast.10, s32[1,128]{1,0:T(1,128)} %bitcast.16, bf16[4,256]{1,0:T(4,128)(2,1)} %table.1, s32[8,32]{1,0:T(8,128)} %bitcast.13, f32[1,256]{1,0:T(1,128)} %bitcast.14, f32[4,8,256]{2,1,0:T(8,128)} %master.1, s32[64,128]{1,0:T(8,128)} %bitcast.11, ...), custom_call_target="tpu_custom_call" | custom-call | tf_op jit(solution)/shard_map/step/pallas_call | solution.py:327
  57.7 0.0 copy-done
  57.7 0.0 copy-done.1
  57.7 1.4 %add_divide_fusion = (f32[4,8,256]{2,1,0:T(8,128)}, f32[4,8,256]{2,1,0:T(8,128)}, f32[4,8,256]{2,1,0:T(8,128)}) fusion(f32[4,8,256]{2,1,0:T(8,128)} %get-tuple-element.7, f32[4,8,256]{2,1,0:T(8,128)S(1)} %copy-done, f32[4,8,256]{2,1,0:T(8,128)S(1)} %copy-done.1), kind=kLoop, calls=%fused_computation.2 | loop fusion | flops 73728 | bytes 196608 | tf_op jit(solution)/shard_map/div | solution.py:378
  59.1 0.0 copy-start.2
  59.1 0.7 %copy-done.2 = f32[1,128]{1,0:T(1,128)S(1)} copy-done((f32[1,128]{1,0:T(1,128)S(1)}, f32[1,128]{1,0:T(1,128)}, u32[]{:S(2)}) %copy-start.2) | copy-done | bytes 536
  59.8 0.5 copy.19
Async XLA Ops:
  0.6 57.1 %copy-start = (f32[4,8,256]{2,1,0:T(8,128)S(1)}, f32[4,8,256]{2,1,0:T(8,128)}, u32[]{:S(2)}) copy-start(f32[4,8,256]{2,1,0:T(8,128)} %param.27) | copy-start | bytes 98308
  0.6 57.1 %copy-start.1 = (f32[4,8,256]{2,1,0:T(8,128)S(1)}, f32[4,8,256]{2,1,0:T(8,128)}, u32[]{:S(2)}) copy-start(f32[4,8,256]{2,1,0:T(8,128)} %param.26) | copy-start | bytes 98308
  59.1 0.7 %copy-start.2 = (f32[1,128]{1,0:T(1,128)S(1)}, f32[1,128]{1,0:T(1,128)}, u32[]{:S(2)}) copy-start(f32[1,128]{1,0:T(1,128)} %get-tuple-element.6) | copy-start | bytes 1540

commit v3 on v2

--- a/solution.py
+++ b/solution.py
@@ -40,23 +40,60 @@
     return {"cell": cell, "brick": brick}
 
 
-def step_kernel(feat, spec, table, sends, gain, master, nbr, cnt, dist, decay, readout, target,
+def step_kernel(master_h, feat_h, spec_h, table_h, gain_h, sends_h, nbr_h, cnt_h, dist_h, decay_h, readout_h, target_h,
                 energy, out,
+                master, feat, spec, table, gain, sends, nbr, cnt, dist, decay, readout, target, sem_in,
                 emb, nt, wa, wb, parcel,
                 idx, dst8, rep, qm, gm, big, att, lmat, onehot, pt_hi, pt_lo, idx2,
-                gtmp, gsend, r1, s2f, s2, r2, fin,
+                n_t, gtmp, gsend, r1, s2f, s2, r2, fin,
                 sem_a, sem_b, sem_g, sem_1, sem_2, sem_3):
     c = lax.axis_index("cell")
     b = lax.axis_index("brick")
     partner = c + 1 - 2 * lax.rem(c, 2)
+    loads = []
+    for i, (src, dst) in enumerate((
+            (master_h, master), (feat_h, feat), (spec_h, spec), (table_h, table), (gain_h, gain), (sends_h, sends),
+            (nbr_h, nbr), (cnt_h, cnt), (dist_h, dist), (decay_h, decay), (readout_h, readout), (target_h, target))):
+        cp = pltpu.make_async_copy(src, dst, sem_in.at[i])
+        cp.start()
+        loads.append(cp)
     barrier = pltpu.get_barrier_semaphore()
     for k in range(1, CELLS):
         pl.semaphore_signal(barrier, inc=1, device_id=peer(lax.rem(c + k, CELLS), b), device_id_type=MESH)
     for d in range(1, BRICKS):
         pl.semaphore_signal(barrier, inc=1, device_id=peer(c, lax.rem(b + d, BRICKS)), device_id_type=MESH)
 
+    loads[0].wait()
     wa[c] = master[0:2].reshape(16, C).astype(bf16)
     wb[c] = master[2:4].reshape(16, C).astype(bf16)
+    pl.semaphore_wait(barrier, CELLS - 1 + BRICKS - 1)
+
+    def same_core(w, sem):
+        made = []
+        for k in range(1, 16):
+            cp = pltpu.make_async_remote_copy(
+                src_ref=w.at[c], dst_ref=w.at[c], send_sem=sem.at[0, k], recv_sem=sem.at[1, k],
+                device_id=peer(lax.rem(c + 2 * k, CELLS), b), device_id_type=MESH)
+            cp.start()
+            made.append(cp)
+        return made
+
+    def forward(w, sem, made):
+        sent = []
+        for k in range(16):
+            if k:
+                made[k - 1].wait_recv()
+            owner = lax.rem(c - 2 * k + CELLS, CELLS)
+            cp = pltpu.make_async_remote_copy(
+                src_ref=w.at[owner], dst_ref=w.at[owner], send_sem=sem.at[2, k], recv_sem=sem.at[3, k],
+                device_id=peer(partner, b), device_id_type=MESH)
+            cp.start()
+            sent.append(cp)
+        return sent
+
+    made_a = same_core(wa, sem_a)
+    for cp in loads[1:6]:
+        cp.wait()
     eye = lax.broadcasted_iota(jnp.int32, (A, A), 0) == lax.broadcasted_iota(jnp.int32, (A, A), 1)
     col = jnp.sum(jnp.where(eye, jnp.broadcast_to(spec[...], (A, A)), 0).astype(f32), axis=1, keepdims=True)
     e = feat[...].astype(f32)
@@ -74,32 +111,6 @@
         take = (row_id == sends[d : d + 1, :]).astype(f32).astype(bf16)
         parcel[d] = dot(take, n, TN).astype(bf16)
     nt[pl.ds(pl.multiple_of(A + 32 * b, 32), 32), :] = parcel[b]
-    pl.semaphore_wait(barrier, CELLS - 1 + BRICKS - 1)
-
-    def same_core(w, sem):
-        made = []
-        for k in range(1, 16):
-            cp = pltpu.make_async_remote_copy(
-                src_ref=w.at[c], dst_ref=w.at[c], send_sem=sem.at[0, k], recv_sem=sem.at[1, k],
-                device_id=peer(lax.rem(c + 2 * k, CELLS), b), device_id_type=MESH)
-            cp.start()
-            made.append(cp)
-        return made
-
-    def forward(w, sem, made):
-        sent = []
-        for k in range(16):
-            if k:
-                made[k - 1].wait_recv()
-            owner = lax.rem(c - 2 * k + CELLS, CELLS)
-            cp = pltpu.make_async_remote_copy(
-                src_ref=w.at[owner], dst_ref=w.at[owner], send_sem=sem.at[2, k], recv_sem=sem.at[3, k],
-                device_id=peer(partner, b), device_id_type=MESH)
-            cp.start()
-            sent.append(cp)
-        return sent
-
-    made_a = same_core(wa, sem_a)
     ghosts = []
     for d in range(1, BRICKS):
         to = lax.rem(b + d, BRICKS)
@@ -111,6 +122,8 @@
         cp.start()
         ghosts.append(cp)
     made_b = same_core(wb, sem_b)
+    for cp in loads[6:]:
+        cp.wait()
 
     scale = 1.0 / math.sqrt(C // H)
     rows = A * H
@@ -124,7 +137,7 @@
     for h in range(H):
         idx[pl.ds(h, A, stride=8), :] = m2
         dst8[pl.ds(h, A, stride=8), :] = d2
-    lmat[...] = jnp.zeros((128, 1024), bf16)
+    lmat[...] = jnp.zeros((8, 128, 1024), bf16)
     t_row = lax.broadcasted_iota(jnp.int32, (T, 128), 0)
     lane8 = lax.broadcasted_iota(jnp.int32, (8, 128), 1)
 
@@ -137,9 +150,10 @@
             hit = t_row == pair[t : t + 1, :]
             onehot[s, :, 128 * t : 128 * t + 128] = jnp.where(hit, 1.0, 0.0).astype(bf16)
 
-    sent_a = forward(wa, sem_a, made_a)
     for cp in ghosts:
         cp.wait()
+    n_t[...] = nt[...].astype(f32).T.astype(bf16)
+    sent_a = forward(wa, sem_a, made_a)
     for cp in sent_a:
         cp.wait_recv()
 
@@ -171,11 +185,11 @@
     sub_head = lax.rem(row_in, 8)
     dec = jnp.zeros((128, 128), f32)
     for h in range(H):
-        dec = jnp.where(sub_head == h, decay[h], dec)
+        dec = jnp.where(sub_head == h, decay[:, h : h + 1], dec)
     diag = lax.rem(row_in // 8, 2) == lane // 64
 
     def pick(s):
-        r0 = pl.multiple_of(s * 128, 128)
+        r0 = s * 128
         ix = idx[pl.ds(r0, 128), :]
         low = jnp.bitwise_and(ix, 127)
         res = jnp.zeros((128, 128), f32)
@@ -187,15 +201,15 @@
     def scatter(s, w32):
         kept = jnp.where(diag, w32, 0.0).astype(bf16)
         for t in range(8):
-            lmat[16 * t : 16 * t + 16, 128 * t : 128 * t + 128] = kept[16 * t : 16 * t + 16, :]
-        hi, lo = split(dot(onehot[s], lmat[...], NT))
-        c0 = pl.multiple_of(s * 128, 128)
-        pt_hi[:, pl.ds(c0, 128)] = hi
-        pt_lo[:, pl.ds(c0, 128)] = lo
-
-    @pl.loop(0, 8)
-    def _(s):
-        r0 = pl.multiple_of(s * 128, 128)
+            lmat[s, 16 * t : 16 * t + 16, 128 * t : 128 * t + 128] = kept[16 * t : 16 * t + 16, :]
+
+    def collect_rows(s):
+        hi, lo = split(dot(onehot[s], lmat[s], NT))
+        pt_hi[:, 128 * s : 128 * s + 128] = hi
+        pt_lo[:, 128 * s : 128 * s + 128] = lo
+
+    for s in range(8):
+        r0 = s * 128
         got, ok = pick(s)
         score = got * scale - dec * dst8[pl.ds(r0, 128), :]
         score = jnp.where(ok, score, -1e30)
@@ -204,6 +218,9 @@
         a = ex / (jnp.sum(ex, axis=1, keepdims=True) * 0.5)
         att[pl.ds(r0, 128), :] = a
         scatter(s, a)
+        if s:
+            collect_rows(s - 1)
+    collect_rows(7)
 
     for cp in sent_b:
         cp.wait_recv()
@@ -260,21 +277,23 @@
         if mult is not None:
             tg = tg * mult
         hi, lo = split(tg)
-        return dot(n_all, hi, TN) + dot(n_all, lo, TN)
+        return dot(n_t[...], hi, NN) + dot(n_t[...], lo, NN)
 
     put(2, table_grad(gm[...], None))
 
-    @pl.loop(0, 8)
-    def _(s):
-        r0 = pl.multiple_of(s * 128, 128)
+    for s in range(8):
+        r0 = s * 128
         gw, ok = pick(s)
         a = att[pl.ds(r0, 128), :]
         mean = jnp.sum(a * gw, axis=1, keepdims=True) * 0.5
         scatter(s, a * (gw - mean))
+        if s:
+            collect_rows(s - 1)
+    collect_rows(7)
 
     put(1, table_grad(qm[...], scale))
     grad_query = gather_heads(k.astype(f32).T.astype(bf16), scale)
-    put(0, dot(n_own, grad_query, TN))
+    put(0, dot(n_t[:, 0:A], grad_query, NN))
 
     for m in (3, 2, 1, 0):
         total = gsend[m, b].astype(f32)
@@ -321,15 +340,27 @@
 
 def step(*args):
     vm = pl.BlockSpec(memory_space=pltpu.VMEM)
-    sm = pl.BlockSpec(memory_space=pltpu.SMEM)
     rows = A * H
     dma = pltpu.SemaphoreType.DMA
     return pl.pallas_call(
         step_kernel,
         out_shape=(jax.ShapeDtypeStruct((1, A), f32), jax.ShapeDtypeStruct((4, 8, C), f32)),
-        in_specs=[vm] * 9 + [sm] + [vm] * 2,
+        in_specs=[pl.BlockSpec(memory_space=pl.ANY)] * 12,
         out_specs=(vm, vm),
         scratch_shapes=[
+            pltpu.VMEM((4, 8, C), f32),
+            pltpu.VMEM((A, C), bf16),
+            pltpu.VMEM((1, A), jnp.int32),
+            pltpu.VMEM((4, C), bf16),
+            pltpu.VMEM((1, C), f32),
+            pltpu.VMEM((BRICKS, 32), jnp.int32),
+            pltpu.VMEM((K, A), jnp.int32),
+            pltpu.VMEM((1, A), jnp.int32),
+            pltpu.VMEM((K, A), f32),
+            pltpu.VMEM((1, H), f32),
+            pltpu.VMEM((1, C), f32),
+            pltpu.VMEM((1, A), f32),
+            dma((12,)),
             pltpu.VMEM((A, C), f32),
             pltpu.VMEM((T, C), bf16),
             pltpu.VMEM((CELLS, 16, C), bf16),
@@ -342,11 +373,12 @@
             pltpu.VMEM((rows, C), bf16),
             pltpu.VMEM((rows, T), f32),
             pltpu.VMEM((rows, 128), f32),
-            pltpu.VMEM((128, 1024), bf16),
+            pltpu.VMEM((8, 128, 1024), bf16),
             pltpu.VMEM((8, T, 1024), bf16),
             pltpu.VMEM((T, rows), bf16),
             pltpu.VMEM((T, rows), bf16),
             pltpu.VMEM((A, 128), jnp.int32),
+            pltpu.VMEM((C, T), bf16),
             pltpu.VMEM((2 * C, 128), f32),
             pltpu.VMEM((4, BRICKS, CELLS, C), bf16),
             pltpu.VMEM((4, BRICKS, CELLS, C), bf16),
@@ -366,17 +398,37 @@
     )(*args)
 
 
+def update_kernel(energy, owned, moment, second, energy_out, moment_out, second_out, step_out):
+    g = owned[...]
+    m = 0.9 * moment[...] + 0.1 * g
+    s = 0.999 * second[...] + 0.001 * g * g
+    moment_out[...] = m
+    second_out[...] = s
+    step_out[...] = m / (jnp.sqrt(s) + 1e-08)
+    energy_out[...] = energy[...]
+
+
+def update(energy, owned, moment, second):
+    vm = pl.BlockSpec(memory_space=pltpu.VMEM)
+    block = jax.ShapeDtypeStruct((4, 8, C), f32)
+    return pl.pallas_call(
+        update_kernel,
+        out_shape=(jax.ShapeDtypeStruct((1, A), f32), block, block, block),
+        in_specs=[vm] * 4,
+        out_specs=(vm,) * 4,
+        name="update",
+    )(energy, owned, moment, second)
+
+
 def body(features, species, species_table, neighbours, counts, send_lists, distances,
          head_decay, norm_gain, readout, targets, master, moment, second):
     energy, owned = step(
-        features.reshape(A, C), species.reshape(1, A), species_table,
-        send_lists.reshape(BRICKS, 32), norm_gain.reshape(1, C), master,
+        master, features.reshape(A, C), species.reshape(1, A), species_table,
+        norm_gain.reshape(1, C), send_lists.reshape(BRICKS, 32),
         neighbours.reshape(K, A), counts.reshape(1, A), distances.reshape(K, A),
-        head_decay, readout.reshape(1, C), targets.reshape(1, A))
-    moment_new = 0.9 * moment + 0.1 * owned
-    second_new = 0.999 * second + 0.001 * owned * owned
-    adam_step = moment_new / (jnp.sqrt(second_new) + 1e-08)
-    return (energy.reshape(1, 1, A), moment_new, second_new, adam_step)
+        head_decay.reshape(1, H), readout.reshape(1, C), targets.reshape(1, A))
+    energies, moment_new, second_new, adam_step = update(energy, owned, moment, second)
+    return (energies.reshape(1, 1, A), moment_new, second_new, adam_step)
 
 
 def solution(mesh):

time: 60.5 us -> 54.5 us (0.901)
  Pallas kernels: 57 us -> 53.7 us
  other arithmetic: 1.4 us -> 0 us
  local copies, waits for them, and re-layouts: 1.2 us -> 0 us
    pallas_call x1, Pallas kernels: 57 us -> 52.2 us  [step(): pl.pallas_call(step_kernel, out_shape=(jax.ShapeDtypeStruct((1, A), f32),...]
    pallas_call x0 -> x1, Pallas kernels: none -> 1.45 us  [update(): pl.pallas_call(update_kernel, out_shape=(jax.ShapeDtypeStruct((1, A), f32...]
    div x1 -> x0, other arithmetic: 1.4 us -> none  [body(): adam_step = moment_new / (jnp.sqrt(second_new) + 1e-08)]
    unnamed x7 -> x0, local copies, waits for them, and re-layouts: 1.2 us -> none
where the time goes in v3:
time: 54.5 us; the launch traced here: 54.3 us
  Pallas kernels  53.7 us (99%)
  between operations  0.64 us (1%)
    pallas_call x1, Pallas kernels, step(): pl.pallas_call(step_kernel, out_shape=(jax.ShapeDtypeStruct((1, A), f32),...  52.2 us
    pallas_call x1, Pallas kernels, update(): pl.pallas_call(update_kernel, out_shape=(jax.ShapeDtypeStruct((1, A), f32...  1.45 us

profile of v3, /device:TPU:1, one launch (start us, length us, event | category | flops | bytes accessed | tf_op | source)
XLA Modules:
  0.0 54.3 jit_solution(2076651940611682073)
XLA Ops:
  0.6 52.2 %step.1 = (f32[1,128]{1,0:T(1,128)}, f32[4,8,256]{2,1,0:T(8,128)}) custom-call(f32[4,8,256]{2,1,0:T(8,128)} %master_h.1, bf16[128,256]{1,0:T(8,128)(2,1)} %bitcast.11, s32[1,128]{1,0:T(1,128)} %bitcast.17, bf16[4,256]{1,0:T(4,128)(2,1)} %table_h.1, f32[1,256]{1,0:T(1,128)} %bitcast.15, s32[8,32]{1,0:T(8,128)} %bitcast.14, s32[64,128]{1,0:T(8,128)} %bitcast.12, ...), custom_call_target="tpu_custom_call" | custom-call | tf_op jit(solution)/shard_map/step/pallas_call | solution.py:345
  52.8 1.4 %update.1 = (f32[1,128]{1,0:T(1,128)}, f32[4,8,256]{2,1,0:T(8,128)}, f32[4,8,256]{2,1,0:T(8,128)}, f32[4,8,256]{2,1,0:T(8,128)}) custom-call(f32[1,128]{1,0:T(1,128)} %get-tuple-element.10.energy, f32[4,8,256]{2,1,0:T(8,128)} %get-tuple-element.11.owned, f32[4,8,256]{2,1,0:T(8,128)} %moment.1, f32[4,8,256]{2,1,0:T(8,128)} %second.1), custom_call_target="tpu_custom_call" | custom-call | tf_op jit(solution)/shard_map/update/pallas_call | solution.py:414

commit v4 on v3

--- a/solution.py
+++ b/solution.py
@@ -58,40 +58,63 @@
         cp.start()
         loads.append(cp)
     barrier = pltpu.get_barrier_semaphore()
-    for k in range(1, CELLS):
-        pl.semaphore_signal(barrier, inc=1, device_id=peer(lax.rem(c + k, CELLS), b), device_id_type=MESH)
-    for d in range(1, BRICKS):
-        pl.semaphore_signal(barrier, inc=1, device_id=peer(c, lax.rem(b + d, BRICKS)), device_id_type=MESH)
-
+    low = lax.rem(c, 16)
+    base = c - low
+    other = 16 - base
+
+    def at(dz, flip):
+        return lax.rem(low + 2 * dz + 16, 16) + (other if flip else base)
+
+    def column(flip):
+        return b + 1 - 2 * lax.rem(b, 2) if flip else b
+
+    spots = [(1, 0), (1, 1), (2, 0), (2, 1), (-1, 0), (-1, 1), (-2, 0), (-2, 1), (0, 1)]
+    hops = [(2, -1, 0), (2, -1, 1), (2, -2, 0), (2, -2, 1), (-2, 1, 0), (-2, 1, 1)]
+
+    def plane(i):
+        return peer(at(0, i // 8), lax.rem(b + i % 8, BRICKS))
+
+    for i in range(1, 16):
+        pl.semaphore_signal(barrier, inc=1, device_id=plane(i), device_id_type=MESH)
+    for dz, flip in spots[:8]:
+        pl.semaphore_signal(barrier, inc=1, device_id=peer(at(dz, flip), column(flip)), device_id_type=MESH)
+    pl.semaphore_signal(barrier, inc=1, device_id=peer(partner, b), device_id_type=MESH)
     loads[0].wait()
     wa[c] = master[0:2].reshape(16, C).astype(bf16)
     wb[c] = master[2:4].reshape(16, C).astype(bf16)
-    pl.semaphore_wait(barrier, CELLS - 1 + BRICKS - 1)
-
-    def same_core(w, sem):
-        made = []
-        for k in range(1, 16):
-            cp = pltpu.make_async_remote_copy(
-                src_ref=w.at[c], dst_ref=w.at[c], send_sem=sem.at[0, k], recv_sem=sem.at[1, k],
-                device_id=peer(lax.rem(c + 2 * k, CELLS), b), device_id_type=MESH)
-            cp.start()
-            made.append(cp)
-        return made
-
-    def forward(w, sem, made):
-        sent = []
-        for k in range(16):
-            if k:
-                made[k - 1].wait_recv()
-            owner = lax.rem(c - 2 * k + CELLS, CELLS)
-            cp = pltpu.make_async_remote_copy(
-                src_ref=w.at[owner], dst_ref=w.at[owner], send_sem=sem.at[2, k], recv_sem=sem.at[3, k],
-                device_id=peer(partner, b), device_id_type=MESH)
-            cp.start()
-            sent.append(cp)
-        return sent
-
-    made_a = same_core(wa, sem_a)
+    pl.semaphore_wait(barrier, 24)
+
+    def send(w, sem, half, i, block, cell, brick):
+        cp = pltpu.make_async_remote_copy(
+            src_ref=w.at[block], dst_ref=w.at[block], send_sem=sem.at[half, i], recv_sem=sem.at[half + 1, i],
+            device_id=peer(cell, brick), device_id_type=MESH)
+        cp.start()
+        return cp
+
+    def share(w, sem, i, block):
+        return send(w, sem, 2, i, block, partner, b)
+
+    def start_near(w, sem):
+        near = [send(w, sem, 0, i, c, at(dz, flip), column(flip)) for i, (dz, flip) in enumerate(spots)]
+        return near, [share(w, sem, 15, c)]
+
+    def relay(w, sem, near, shared):
+        far = []
+        for i, (dz, flip) in enumerate(spots):
+            near[i].wait_recv()
+            block = at(-dz, flip)
+            for j, (to, off, kind) in enumerate(hops):
+                if (-dz, flip) == (off, kind):
+                    far.append(send(w, sem, 0, 9 + j, block, at(to, 0), b))
+            shared.append(share(w, sem, i, block))
+        return far
+
+    def finish(w, sem, far, shared):
+        for j, (to, off, kind) in enumerate(hops):
+            far[j].wait_recv()
+            shared.append(share(w, sem, 9 + j, at(off - to, kind)))
+
+    near_a, shared_a = start_near(wa, sem_a)
     for cp in loads[1:6]:
         cp.wait()
     eye = lax.broadcasted_iota(jnp.int32, (A, A), 0) == lax.broadcasted_iota(jnp.int32, (A, A), 1)
@@ -121,7 +144,7 @@
             device_id=peer(c, to), device_id_type=MESH)
         cp.start()
         ghosts.append(cp)
-    made_b = same_core(wb, sem_b)
+    near_b, shared_b = start_near(wb, sem_b)
     for cp in loads[6:]:
         cp.wait()
 
@@ -138,6 +161,8 @@
         idx[pl.ds(h, A, stride=8), :] = m2
         dst8[pl.ds(h, A, stride=8), :] = d2
     lmat[...] = jnp.zeros((8, 128, 1024), bf16)
+    far_a = relay(wa, sem_a, near_a, shared_a)
+    far_b = relay(wb, sem_b, near_b, shared_b)
     t_row = lax.broadcasted_iota(jnp.int32, (T, 128), 0)
     lane8 = lax.broadcasted_iota(jnp.int32, (8, 128), 1)
 
@@ -150,11 +175,11 @@
             hit = t_row == pair[t : t + 1, :]
             onehot[s, :, 128 * t : 128 * t + 128] = jnp.where(hit, 1.0, 0.0).astype(bf16)
 
+    finish(wa, sem_a, far_a, shared_a)
     for cp in ghosts:
         cp.wait()
     n_t[...] = nt[...].astype(f32).T.astype(bf16)
-    sent_a = forward(wa, sem_a, made_a)
-    for cp in sent_a:
+    for cp in shared_a:
         cp.wait_recv()
 
     def weight(w, m):
@@ -178,7 +203,7 @@
 
     qm[...] = spread_heads(q.astype(f32))
     big[...] = dot(qm[...], k, NT)
-    sent_b = forward(wb, sem_b, made_b)
+    finish(wb, sem_b, far_b, shared_b)
 
     lane = lax.broadcasted_iota(jnp.int32, (128, 128), 1)
     row_in = lax.broadcasted_iota(jnp.int32, (128, 128), 0)
@@ -222,7 +247,7 @@
             collect_rows(s - 1)
     collect_rows(7)
 
-    for cp in sent_b:
+    for cp in shared_b:
         cp.wait_recv()
     w_o = weight(wb, 1)
     v = dot(n_all, weight(wb, 0), NN).astype(bf16)
@@ -259,11 +284,12 @@
             gsend[m, d] = jnp.concatenate(
                 [gtmp[pl.ds(d, CELLS, stride=8), :], gtmp[pl.ds(C + d, CELLS, stride=8), :]], axis=1).astype(bf16)
         made = []
-        for d in range(1, BRICKS):
-            to = lax.rem(b + d, BRICKS)
+        for i in range(1, 16):
+            half = pl.ds(pl.multiple_of(other if i // 8 else base, 16), 16)
             cp = pltpu.make_async_remote_copy(
-                src_ref=gsend.at[m, to], dst_ref=r1.at[m, b], send_sem=sem_1.at[m, 0, d], recv_sem=sem_1.at[m, 1, d],
-                device_id=peer(c, to), device_id_type=MESH)
+                src_ref=gsend.at[m, lax.rem(b + i % 8, BRICKS), half, :], dst_ref=r1.at[m, base // 2 + b],
+                send_sem=sem_1.at[m, 0, i], recv_sem=sem_1.at[m, 1, i],
+                device_id=plane(i), device_id_type=MESH)
             cp.start()
             made.append(cp)
         first[m] = made
@@ -296,24 +322,25 @@
     put(0, dot(n_t[:, 0:A], grad_query, NN))
 
     for m in (3, 2, 1, 0):
-        total = gsend[m, b].astype(f32)
-        for d in range(1, BRICKS):
-            first[m][d - 1].wait_recv()
-            total = total + r1[m, lax.rem(b - d + BRICKS, BRICKS)].astype(f32)
-        s2f[pl.ds(2 * m, CELLS, stride=8), :] = total[:, 0:128]
-        s2f[pl.ds(2 * m + 1, CELLS, stride=8), :] = total[:, 128:256]
-    s2[...] = s2f[...].reshape(CELLS, 8, 128).astype(bf16)
+        total = gsend[m, b, pl.ds(pl.multiple_of(base, 16), 16), :].astype(f32)
+        for i in range(1, 16):
+            first[m][i - 1].wait_recv()
+            source = (other if i // 8 else base) // 2 + lax.rem(b - i % 8 + BRICKS, BRICKS)
+            total = total + r1[m, source].astype(f32)
+        s2f[pl.ds(2 * m, 16, stride=8), :] = total[:, 0:128]
+        s2f[pl.ds(2 * m + 1, 16, stride=8), :] = total[:, 128:256]
+    s2[...] = s2f[...].reshape(16, 8, 128).astype(bf16)
 
     second = []
-    for k in range(1, CELLS):
-        to = lax.rem(c + k, CELLS)
+    for k in range(1, 16):
+        to = lax.rem(low + k, 16)
         cp = pltpu.make_async_remote_copy(
-            src_ref=s2.at[to], dst_ref=r2.at[c], send_sem=sem_2.at[0, k], recv_sem=sem_2.at[1, k],
-            device_id=peer(to, b), device_id_type=MESH)
+            src_ref=s2.at[to], dst_ref=r2.at[low], send_sem=sem_2.at[0, k], recv_sem=sem_2.at[1, k],
+            device_id=peer(base + to, b), device_id_type=MESH)
         cp.start()
         second.append(cp)
-    r2[c] = s2[c]
-    for cp in made_a + made_b + sent_a + sent_b:
+    r2[low] = s2[low]
+    for cp in near_a + near_b + far_a + far_b + shared_a + shared_b:
         cp.wait_send()
     for m in range(4):
         for cp in first[m]:
@@ -381,16 +408,16 @@
             pltpu.VMEM((C, T), bf16),
             pltpu.VMEM((2 * C, 128), f32),
             pltpu.VMEM((4, BRICKS, CELLS, C), bf16),
-            pltpu.VMEM((4, BRICKS, CELLS, C), bf16),
-            pltpu.VMEM((CELLS * 8, 128), f32),
-            pltpu.VMEM((CELLS, 8, 128), bf16),
-            pltpu.VMEM((CELLS, 8, 128), bf16),
+            pltpu.VMEM((4, 16, 16, C), bf16),
+            pltpu.VMEM((128, 128), f32),
+            pltpu.VMEM((16, 8, 128), bf16),
+            pltpu.VMEM((16, 8, 128), bf16),
             pltpu.VMEM((BRICKS * 8, 128), f32),
             dma((4, 16)),
             dma((4, 16)),
             dma((2, BRICKS)),
-            dma((4, 2, BRICKS)),
-            dma((2, CELLS)),
+            dma((4, 2, 16)),
+            dma((2, 16)),
             dma((2, BRICKS)),
         ],
         compiler_params=pltpu.CompilerParams(collective_id=0, has_side_effects=True),

time: 54.5 us -> 52.9 us (0.971)
  Pallas kernels: 53.7 us -> 52.1 us
    pallas_call x1, Pallas kernels: 52.2 us -> 50.6 us  [step(): pl.pallas_call(step_kernel, out_shape=(jax.ShapeDtypeStruct((1, A), f32),...]
where the time goes in v4:
time: 52.9 us; the launch traced here: 52.7 us
  Pallas kernels  52.1 us (98%)
  between operations  0.64 us (1%)
    pallas_call x1, Pallas kernels, step(): pl.pallas_call(step_kernel, out_shape=(jax.ShapeDtypeStruct((1, A), f32),...  50.6 us
    pallas_call x1, Pallas kernels, update(): pl.pallas_call(update_kernel, out_shape=(jax.ShapeDtypeStruct((1, A), f32...  1.45 us

profile of v4, /device:TPU:1, one launch (start us, length us, event | category | flops | bytes accessed | tf_op | source)
XLA Modules:
  0.0 52.7 jit_solution(7008396487569217282)
XLA Ops:
  0.6 50.6 %step.1 = (f32[1,128]{1,0:T(1,128)}, f32[4,8,256]{2,1,0:T(8,128)}) custom-call(f32[4,8,256]{2,1,0:T(8,128)} %master_h.1, bf16[128,256]{1,0:T(8,128)(2,1)} %bitcast.11, s32[1,128]{1,0:T(1,128)} %bitcast.17, bf16[4,256]{1,0:T(4,128)(2,1)} %table_h.1, f32[1,256]{1,0:T(1,128)} %bitcast.15, s32[8,32]{1,0:T(8,128)} %bitcast.14, s32[64,128]{1,0:T(8,128)} %bitcast.12, ...), custom_call_target="tpu_custom_call" | custom-call | tf_op jit(solution)/shard_map/step/pallas_call | solution.py:372
  51.2 1.4 %update.1 = (f32[1,128]{1,0:T(1,128)}, f32[4,8,256]{2,1,0:T(8,128)}, f32[4,8,256]{2,1,0:T(8,128)}, f32[4,8,256]{2,1,0:T(8,128)}) custom-call(f32[1,128]{1,0:T(1,128)} %get-tuple-element.10.energy, f32[4,8,256]{2,1,0:T(8,128)} %get-tuple-element.11.owned, f32[4,8,256]{2,1,0:T(8,128)} %moment.1, f32[4,8,256]{2,1,0:T(8,128)} %second.1), custom_call_target="tpu_custom_call" | custom-call | tf_op jit(solution)/shard_map/update/pallas_call | solution.py:441

commit v5 on v4

--- a/solution.py
+++ b/solution.py
@@ -44,7 +44,7 @@
                 energy, out,
                 master, feat, spec, table, gain, sends, nbr, cnt, dist, decay, readout, target, sem_in,
                 emb, nt, wa, wb, parcel,
-                idx, dst8, rep, qm, gm, big, att, lmat, onehot, pt_hi, pt_lo, idx2,
+                idx, dst8, rep, qm, gm, qm_t, gm_t, big, att, onehot, p2, msk, k2, v2,
                 n_t, gtmp, gsend, r1, s2f, s2, r2, fin,
                 sem_a, sem_b, sem_g, sem_1, sem_2, sem_3):
     c = lax.axis_index("cell")
@@ -156,29 +156,26 @@
     d_t = dist[...].T
     m2 = jnp.concatenate([m_t, m_t], axis=1)
     d2 = jnp.concatenate([d_t, d_t], axis=1)
-    idx2[...] = m2
+    msk[...] = jnp.bitwise_and(masked, 127)
     for h in range(H):
         idx[pl.ds(h, A, stride=8), :] = m2
         dst8[pl.ds(h, A, stride=8), :] = d2
-    lmat[...] = jnp.zeros((8, 128, 1024), bf16)
     far_a = relay(wa, sem_a, near_a, shared_a)
     far_b = relay(wb, sem_b, near_b, shared_b)
-    t_row = lax.broadcasted_iota(jnp.int32, (T, 128), 0)
-    lane8 = lax.broadcasted_iota(jnp.int32, (8, 128), 1)
-
-    @pl.loop(0, 8)
-    def _(s):
-        ev = idx2[pl.ds(16 * s, 8, stride=2), :]
-        od = idx2[pl.ds(16 * s + 1, 8, stride=2), :]
-        pair = jnp.where(lane8 < 64, ev, od)
-        for t in range(8):
-            hit = t_row == pair[t : t + 1, :]
-            onehot[s, :, 128 * t : 128 * t + 128] = jnp.where(hit, 1.0, 0.0).astype(bf16)
+    lane64 = lax.broadcasted_iota(jnp.int32, (K, 128), 1)
+
+    @pl.loop(0, A // 4)
+    def _(g):
+        for i in range(4):
+            column_a = jnp.take_along_axis(msk[...], jnp.full((K, 128), 4 * g + i, jnp.int32), axis=1)
+            onehot[g, 64 * i : 64 * i + 64, :] = jnp.where(column_a == lane64, 1.0, 0.0).astype(bf16)
 
     finish(wa, sem_a, far_a, shared_a)
     for cp in ghosts:
         cp.wait()
-    n_t[...] = nt[...].astype(f32).T.astype(bf16)
+    n_cols = nt[...].astype(f32).T.astype(bf16)
+    n_t[:, 0:T] = n_cols
+    n_t[:, T : 2 * T] = n_cols
     for cp in shared_a:
         cp.wait_recv()
 
@@ -202,6 +199,7 @@
         return jnp.where(head_mask, x, 0.0).astype(bf16)
 
     qm[...] = spread_heads(q.astype(f32))
+    qm_t[...] = qm[...].T
     big[...] = dot(qm[...], k, NT)
     finish(wb, sem_b, far_b, shared_b)
 
@@ -223,15 +221,23 @@
             res = jnp.where(ix >= 128 * t, g, res)
         return res, ix < 512
 
+    blank = jnp.zeros((16, 128), bf16)
+
     def scatter(s, w32):
-        kept = jnp.where(diag, w32, 0.0).astype(bf16)
-        for t in range(8):
-            lmat[s, 16 * t : 16 * t + 16, 128 * t : 128 * t + 128] = kept[16 * t : 16 * t + 16, :]
-
-    def collect_rows(s):
-        hi, lo = split(dot(onehot[s], lmat[s], NT))
-        pt_hi[:, 128 * s : 128 * s + 128] = hi
-        pt_lo[:, 128 * s : 128 * s + 128] = lo
+        kept = jnp.where(diag, w32, 0.0)
+        block = idx[128 * s : 128 * s + 128, :] // 128
+        parts = [jnp.where(block == t, kept, 0.0).astype(bf16) for t in range(3)]
+        dense = []
+        for i in range(4):
+            r = 32 * i
+            left = jnp.concatenate([x[r : r + 16, :] if y == 0 else blank for x in parts for y in range(2)], axis=0)
+            right = jnp.concatenate([blank if y == 0 else x[r + 16 : r + 32, :] for x in parts for y in range(2)], axis=0)
+            dense.append(dot(jnp.concatenate([left, right], axis=1), onehot[4 * s + i], NN))
+        for t in range(3):
+            x = jnp.concatenate([d[32 * t : 32 * t + 32, :] for d in dense], axis=0)
+            hi, lo = split(x)
+            p2[128 * s : 128 * s + 128, 128 * t : 128 * t + 128] = hi
+            p2[128 * s : 128 * s + 128, T + 128 * t : T + 128 * t + 128] = lo
 
     for s in range(8):
         r0 = s * 128
@@ -243,28 +249,27 @@
         a = ex / (jnp.sum(ex, axis=1, keepdims=True) * 0.5)
         att[pl.ds(r0, 128), :] = a
         scatter(s, a)
-        if s:
-            collect_rows(s - 1)
-    collect_rows(7)
 
     for cp in shared_b:
         cp.wait_recv()
     w_o = weight(wb, 1)
     v = dot(n_all, weight(wb, 0), NN).astype(bf16)
 
-    head_sel = (lax.rem(lax.broadcasted_iota(jnp.int32, (C, rows), 1), 8)
-                == lax.broadcasted_iota(jnp.int32, (C, rows), 0) // 32)
     collect = (lax.broadcasted_iota(jnp.int32, (A, rows), 1) // 8
                == lax.broadcasted_iota(jnp.int32, (A, rows), 0)).astype(f32).astype(bf16)
 
-    def gather_heads(table_t, mult):
-        full = dot(table_t, pt_hi[...], NN) + dot(table_t, pt_lo[...], NN)
+    def gather_heads(source, mult):
+        full = dot(p2[...], source[...], NN)
         if mult is not None:
             full = full * mult
-        kept = jnp.where(head_sel, full, 0.0).astype(bf16)
-        return dot(collect, kept, NT).astype(bf16)
-
-    attended = gather_heads(v.astype(f32).T.astype(bf16), None)
+        kept = jnp.where(head_mask, full, 0.0).astype(bf16)
+        return dot(collect, kept, NN).astype(bf16)
+
+    v2[0:T, :] = v
+    v2[T : 2 * T, :] = v
+    k2[0:T, :] = k
+    k2[T : 2 * T, :] = k
+    attended = gather_heads(v2, None)
     updated = emb[...] + dot(attended, w_o, NN)
     sig = jax.nn.sigmoid(updated)
     e_col = jnp.sum(readout[...] * (updated * sig), axis=1, keepdims=True)
@@ -296,16 +301,17 @@
 
     put(3, dot(attended, grad_updated, TN))
     gm[...] = spread_heads(grad_att.astype(f32))
+    gm_t[...] = gm[...].T
     big[...] = dot(gm[...], v, NT)
 
-    def table_grad(rows_m, mult):
-        tg = dot(pt_hi[...], rows_m, NN) + dot(pt_lo[...], rows_m, NN)
+    def table_grad(rows_t, mult):
+        both = dot(rows_t, p2[...], NN)
+        tg = both[:, 0:T] + both[:, T : 2 * T]
         if mult is not None:
             tg = tg * mult
-        hi, lo = split(tg)
-        return dot(n_t[...], hi, NN) + dot(n_t[...], lo, NN)
-
-    put(2, table_grad(gm[...], None))
+        return dot(n_t[...], jnp.concatenate(split(tg), axis=1), NT)
+
+    put(2, table_grad(gm_t[...], None))
 
     for s in range(8):
         r0 = s * 128
@@ -313,12 +319,9 @@
         a = att[pl.ds(r0, 128), :]
         mean = jnp.sum(a * gw, axis=1, keepdims=True) * 0.5
         scatter(s, a * (gw - mean))
-        if s:
-            collect_rows(s - 1)
-    collect_rows(7)
-
-    put(1, table_grad(qm[...], scale))
-    grad_query = gather_heads(k.astype(f32).T.astype(bf16), scale)
+
+    put(1, table_grad(qm_t[...], scale))
+    grad_query = gather_heads(k2, scale)
     put(0, dot(n_t[:, 0:A], grad_query, NN))
 
     for m in (3, 2, 1, 0):
@@ -398,14 +401,16 @@
             pltpu.VMEM((2 * rows, 128), f32),
             pltpu.VMEM((rows, C), bf16),
             pltpu.VMEM((rows, C), bf16),
+            pltpu.VMEM((C, rows), bf16),
+            pltpu.VMEM((C, rows), bf16),
             pltpu.VMEM((rows, T), f32),
             pltpu.VMEM((rows, 128), f32),
-            pltpu.VMEM((8, 128, 1024), bf16),
-            pltpu.VMEM((8, T, 1024), bf16),
-            pltpu.VMEM((T, rows), bf16),
-            pltpu.VMEM((T, rows), bf16),
-            pltpu.VMEM((A, 128), jnp.int32),
-            pltpu.VMEM((C, T), bf16),
+            pltpu.VMEM((A // 4, 256, 128), bf16),
+            pltpu.VMEM((rows, 2 * T), bf16),
+            pltpu.VMEM((K, A), jnp.int32),
+            pltpu.VMEM((2 * T, C), bf16),
+            pltpu.VMEM((2 * T, C), bf16),
+            pltpu.VMEM((C, 2 * T), bf16),
             pltpu.VMEM((2 * C, 128), f32),
             pltpu.VMEM((4, BRICKS, CELLS, C), bf16),
             pltpu.VMEM((4, 16, 16, C), bf16),

time: 52.9 us -> 50.9 us (0.962)
  Pallas kernels: 52.1 us -> 50 us
    pallas_call x1, Pallas kernels: 50.6 us -> 48.6 us  [step(): pl.pallas_call(step_kernel, out_shape=(jax.ShapeDtypeStruct((1, A), f32),...]
where the time goes in v5:
time: 50.9 us; the launch traced here: 50.7 us
  Pallas kernels  50 us (98%)
  between operations  0.64 us (1%)
    pallas_call x1, Pallas kernels, step(): pl.pallas_call(step_kernel, out_shape=(jax.ShapeDtypeStruct((1, A), f32),...  48.6 us
    pallas_call x1, Pallas kernels, update(): pl.pallas_call(update_kernel, out_shape=(jax.ShapeDtypeStruct((1, A), f32...  1.45 us

profile of v5, /device:TPU:1, one launch (start us, length us, event | category | flops | bytes accessed | tf_op | source)
XLA Modules:
  0.0 50.7 jit_solution(16700140763169521992)
XLA Ops:
  0.6 48.6 %step.1 = (f32[1,128]{1,0:T(1,128)}, f32[4,8,256]{2,1,0:T(8,128)}) custom-call(f32[4,8,256]{2,1,0:T(8,128)} %master_h.1, bf16[128,256]{1,0:T(8,128)(2,1)} %bitcast.11, s32[1,128]{1,0:T(1,128)} %bitcast.17, bf16[4,256]{1,0:T(4,128)(2,1)} %table_h.1, f32[1,256]{1,0:T(1,128)} %bitcast.15, s32[8,32]{1,0:T(8,128)} %bitcast.14, s32[64,128]{1,0:T(8,128)} %bitcast.12, ...), custom_call_target="tpu_custom_call" | custom-call | tf_op jit(solution)/shard_map/step/pallas_call | solution.py:375
  49.2 1.4 %update.1 = (f32[1,128]{1,0:T(1,128)}, f32[4,8,256]{2,1,0:T(8,128)}, f32[4,8,256]{2,1,0:T(8,128)}, f32[4,8,256]{2,1,0:T(8,128)}) custom-call(f32[1,128]{1,0:T(1,128)} %get-tuple-element.10.energy, f32[4,8,256]{2,1,0:T(8,128)} %get-tuple-element.11.owned, f32[4,8,256]{2,1,0:T(8,128)} %moment.1, f32[4,8,256]{2,1,0:T(8,128)} %second.1), custom_call_target="tpu_custom_call" | custom-call | tf_op jit(solution)/shard_map/update/pallas_call | solution.py:446

commit v6 on v5

--- a/solution.py
+++ b/solution.py
@@ -374,7 +374,7 @@
     dma = pltpu.SemaphoreType.DMA
     return pl.pallas_call(
         step_kernel,
-        out_shape=(jax.ShapeDtypeStruct((1, A), f32), jax.ShapeDtypeStruct((4, 8, C), f32)),
+        out_shape=(pltpu.VMEM((1, A), f32), pltpu.VMEM((4, 8, C), f32)),
         in_specs=[pl.BlockSpec(memory_space=pl.ANY)] * 12,
         out_specs=(vm, vm),
         scratch_shapes=[
@@ -443,6 +443,10 @@
 def update(energy, owned, moment, second):
     vm = pl.BlockSpec(memory_space=pltpu.VMEM)
     block = jax.ShapeDtypeStruct((4, 8, C), f32)
+    energy = pltpu.with_memory_space_constraint(energy, pltpu.VMEM)
+    owned = pltpu.with_memory_space_constraint(owned, pltpu.VMEM)
+    moment = pltpu.with_memory_space_constraint(moment, pltpu.VMEM)
+    second = pltpu.with_memory_space_constraint(second, pltpu.VMEM)
     return pl.pallas_call(
         update_kernel,
         out_shape=(jax.ShapeDtypeStruct((1, A), f32), block, block, block),

time: 50.9 us -> 49.3 us (0.969)
  Pallas kernels: 50 us -> 48.5 us
    pallas_call x1, Pallas kernels: 1.45 us -> 0.65 us  [update(): pl.pallas_call(update_kernel, out_shape=(jax.ShapeDtypeStruct((1, A), f32...]
    pallas_call x1, Pallas kernels: 48.6 us -> 47.8 us  [step(): pl.pallas_call(step_kernel, out_shape=(pltpu.VMEM((1, A), f32), pltpu.VME...]
where the time goes in v6:
time: 49.3 us; the launch traced here: 49.2 us
  Pallas kernels  48.5 us (98%)
  between operations  0.68 us (1%)
    pallas_call x1, Pallas kernels, step(): pl.pallas_call(step_kernel, out_shape=(pltpu.VMEM((1, A), f32), pltpu.VME...  47.8 us

profile of v6, /device:TPU:1, one launch (start us, length us, event | category | flops | bytes accessed | tf_op | source)
XLA Modules:
  0.0 49.2 jit_solution(8135136716284681554)
XLA Ops:
  0.6 0.0 copy-start
  0.6 0.0 copy-start.1
  0.7 47.8 %step.1 = (f32[1,128]{1,0:T(1,128)S(1)}, f32[4,8,256]{2,1,0:T(8,128)S(1)}) custom-call(f32[4,8,256]{2,1,0:T(8,128)} %master_h.1, bf16[128,256]{1,0:T(8,128)(2,1)} %bitcast.11, s32[1,128]{1,0:T(1,128)} %bitcast.17, bf16[4,256]{1,0:T(4,128)(2,1)} %table_h.1, f32[1,256]{1,0:T(1,128)} %bitcast.15, s32[8,32]{1,0:T(8,128)} %bitcast.14, s32[64,128]{1,0:T(8,128)} %bitcast.12, ...), custom_call_target="tpu_custom_call" | custom-call | tf_op jit(solution)/shard_map/step/pallas_call | solution.py:375
  48.5 0.0 copy-done
  48.5 0.0 copy-done.1
  48.5 0.7 %update.1 = (f32[1,128]{1,0:T(1,128)}, f32[4,8,256]{2,1,0:T(8,128)}, f32[4,8,256]{2,1,0:T(8,128)}, f32[4,8,256]{2,1,0:T(8,128)}) custom-call(f32[1,128]{1,0:T(1,128)S(1)} %get-tuple-element.10.energy, f32[4,8,256]{2,1,0:T(8,128)S(1)} %get-tuple-element.11.owned, f32[4,8,256]{2,1,0:T(8,128)S(1)} %copy-done, f32[4,8,256]{2,1,0:T(8,128)S(1)} %copy-done.1), custom_call_target="tpu_custom_call" | custom-call | tf_op jit(solution)/shard_map/update/pallas_call | solution.py:450
Async XLA Ops:
  0.6 47.9 %copy-start = (f32[4,8,256]{2,1,0:T(8,128)S(1)}, f32[4,8,256]{2,1,0:T(8,128)}, u32[]{:S(2)}) copy-start(f32[4,8,256]{2,1,0:T(8,128)} %moment.1) | copy-start | bytes 98308
  0.6 47.9 %copy-start.1 = (f32[4,8,256]{2,1,0:T(8,128)S(1)}, f32[4,8,256]{2,1,0:T(8,128)}, u32[]{:S(2)}) copy-start(f32[4,8,256]{2,1,0:T(8,128)} %second.1) | copy-start | bytes 98308

commit v7 on v6

--- a/solution.py
+++ b/solution.py
@@ -79,10 +79,13 @@
     for dz, flip in spots[:8]:
         pl.semaphore_signal(barrier, inc=1, device_id=peer(at(dz, flip), column(flip)), device_id_type=MESH)
     pl.semaphore_signal(barrier, inc=1, device_id=peer(partner, b), device_id_type=MESH)
+    for dz in (2, -2):
+        across = at(dz, 0) + 1 - 2 * lax.rem(c, 2)
+        pl.semaphore_signal(barrier, inc=1, device_id=peer(across, b), device_id_type=MESH)
     loads[0].wait()
     wa[c] = master[0:2].reshape(16, C).astype(bf16)
     wb[c] = master[2:4].reshape(16, C).astype(bf16)
-    pl.semaphore_wait(barrier, 24)
+    pl.semaphore_wait(barrier, 26)
 
     def send(w, sem, half, i, block, cell, brick):
         cp = pltpu.make_async_remote_copy(
@@ -98,7 +101,7 @@
         near = [send(w, sem, 0, i, c, at(dz, flip), column(flip)) for i, (dz, flip) in enumerate(spots)]
         return near, [share(w, sem, 15, c)]
 
-    def relay(w, sem, near, shared):
+    def relay(w, sem, near, shared, cross):
         far = []
         for i, (dz, flip) in enumerate(spots):
             near[i].wait_recv()
@@ -106,13 +109,16 @@
             for j, (to, off, kind) in enumerate(hops):
                 if (-dz, flip) == (off, kind):
                     far.append(send(w, sem, 0, 9 + j, block, at(to, 0), b))
+                    if cross:
+                        shared.append(send(w, sem, 2, 9 + j, block, at(to, 0) + 1 - 2 * lax.rem(c, 2), b))
             shared.append(share(w, sem, i, block))
         return far
 
-    def finish(w, sem, far, shared):
+    def finish(w, sem, far, shared, cross):
         for j, (to, off, kind) in enumerate(hops):
             far[j].wait_recv()
-            shared.append(share(w, sem, 9 + j, at(off - to, kind)))
+            if not cross:
+                shared.append(share(w, sem, 9 + j, at(off - to, kind)))
 
     near_a, shared_a = start_near(wa, sem_a)
     for cp in loads[1:6]:
@@ -160,8 +166,8 @@
     for h in range(H):
         idx[pl.ds(h, A, stride=8), :] = m2
         dst8[pl.ds(h, A, stride=8), :] = d2
-    far_a = relay(wa, sem_a, near_a, shared_a)
-    far_b = relay(wb, sem_b, near_b, shared_b)
+    far_a = relay(wa, sem_a, near_a, shared_a, True)
+    far_b = relay(wb, sem_b, near_b, shared_b, False)
     lane64 = lax.broadcasted_iota(jnp.int32, (K, 128), 1)
 
     @pl.loop(0, A // 4)
@@ -170,7 +176,7 @@
             column_a = jnp.take_along_axis(msk[...], jnp.full((K, 128), 4 * g + i, jnp.int32), axis=1)
             onehot[g, 64 * i : 64 * i + 64, :] = jnp.where(column_a == lane64, 1.0, 0.0).astype(bf16)
 
-    finish(wa, sem_a, far_a, shared_a)
+    finish(wa, sem_a, far_a, shared_a, True)
     for cp in ghosts:
         cp.wait()
     n_cols = nt[...].astype(f32).T.astype(bf16)
@@ -201,7 +207,7 @@
     qm[...] = spread_heads(q.astype(f32))
     qm_t[...] = qm[...].T
     big[...] = dot(qm[...], k, NT)
-    finish(wb, sem_b, far_b, shared_b)
+    finish(wb, sem_b, far_b, shared_b, False)
 
     lane = lax.broadcasted_iota(jnp.int32, (128, 128), 1)
     row_in = lax.broadcasted_iota(jnp.int32, (128, 128), 0)

time: 49.3 us -> 48.9 us (level)
  no operation moved by 1% of the time
where the time goes in v7:
time: 48.9 us; the launch traced here: 48.8 us
  Pallas kernels  48.1 us (98%)
  between operations  0.68 us (1%)
    pallas_call x1, Pallas kernels, step(): pl.pallas_call(step_kernel, out_shape=(pltpu.VMEM((1, A), f32), pltpu.VME...  47.4 us

profile of v7, /device:TPU:1, one launch (start us, length us, event | category | flops | bytes accessed | tf_op | source)
XLA Modules:
  0.0 48.8 jit_solution(7327913800155494663)
XLA Ops:
  0.6 0.0 copy-start
  0.6 0.0 copy-start.1
  0.7 47.4 %step.1 = (f32[1,128]{1,0:T(1,128)S(1)}, f32[4,8,256]{2,1,0:T(8,128)S(1)}) custom-call(f32[4,8,256]{2,1,0:T(8,128)} %master_h.1, bf16[128,256]{1,0:T(8,128)(2,1)} %bitcast.11, s32[1,128]{1,0:T(1,128)} %bitcast.17, bf16[4,256]{1,0:T(4,128)(2,1)} %table_h.1, f32[1,256]{1,0:T(1,128)} %bitcast.15, s32[8,32]{1,0:T(8,128)} %bitcast.14, s32[64,128]{1,0:T(8,128)} %bitcast.12, ...), custom_call_target="tpu_custom_call" | custom-call | tf_op jit(solution)/shard_map/step/pallas_call | solution.py:381
  48.1 0.0 copy-done
  48.1 0.0 copy-done.1
  48.1 0.7 %update.1 = (f32[1,128]{1,0:T(1,128)}, f32[4,8,256]{2,1,0:T(8,128)}, f32[4,8,256]{2,1,0:T(8,128)}, f32[4,8,256]{2,1,0:T(8,128)}) custom-call(f32[1,128]{1,0:T(1,128)S(1)} %get-tuple-element.10.energy, f32[4,8,256]{2,1,0:T(8,128)S(1)} %get-tuple-element.11.owned, f32[4,8,256]{2,1,0:T(8,128)S(1)} %copy-done, f32[4,8,256]{2,1,0:T(8,128)S(1)} %copy-done.1), custom_call_target="tpu_custom_call" | custom-call | tf_op jit(solution)/shard_map/update/pallas_call | solution.py:456
Async XLA Ops:
  0.6 47.4 %copy-start = (f32[4,8,256]{2,1,0:T(8,128)S(1)}, f32[4,8,256]{2,1,0:T(8,128)}, u32[]{:S(2)}) copy-start(f32[4,8,256]{2,1,0:T(8,128)} %moment.1) | copy-start | bytes 98308
  0.6 47.4 %copy-start.1 = (f32[4,8,256]{2,1,0:T(8,128)S(1)}, f32[4,8,256]{2,1,0:T(8,128)}, u32[]{:S(2)}) copy-start(f32[4,8,256]{2,1,0:T(8,128)} %second.1) | copy-start | bytes 98308
